TPU v7x, 256 devices: a whole 4x4x8 slice. The times are simulated.
256 devices in a mesh: wide: 32 (over y_lo, z, core), narrow: 8 (over y_hi, x).
Axes of the slice: x: 4, y: 4 (y_hi: 2, y_lo: 2; y = y_hi * 2 + y_lo), z: 8, core: 2. Of those that a mesh axis runs over, the one named last changes fastest.
Arguments:
- vectors: bfloat16 [65536, 768], P(('wide', 'narrow')), may hold values from -15 to 15
- block_sides: int32 [512], P(('wide', 'narrow')), may hold values from 0 to 1, as said below
- centers: bfloat16 [32768, 768], P(('wide', 'narrow')), may hold values from -8.5 to 8.5
Outputs:
- new_centers: bfloat16 [32768, 768], P(('wide', 'narrow'))
Inputs may be any that keep to these rules, and one draw needn't show every extreme that they name: `block_sides`: of the 2 labels of one device (consecutive runs of 2 entries), exactly half are 1.
All inputs are finite; a program needn't handle non-finite values.
Results may differ from a plain program's by a relative error of at most 0.0018.
The roundings to bfloat16 on the way count: a program that leaves them out, or rounds other values in their place, can miss the bound.
Values may be sent and summed in bfloat16 or wider, within the bound.
A program may use at most 64 MiB of HBM per device.

v0:
```python
import math

import jax
import jax.numpy as jnp
from jax import lax
from jax.sharding import PartitionSpec as P

LEVEL = 1
ITERS = 2


def from_partner(value, axis, distance):
    mask = 2**distance
    pairs = [(source, source ^ mask) for source in range(lax.axis_size(axis))]
    return lax.ppermute(value, axis, pairs)


def shifted(value, axis, steps):
    count = lax.axis_size(axis)
    pairs = [(source, (source + steps) % count) for source in range(count)]
    return lax.ppermute(value, axis, pairs)


def combined_all(part, axis, combine):
    gathered = jax.tree.map(lambda a: lax.all_gather(a, axis), part)

    def take(source):
        return jax.tree.map(lambda a: lax.dynamic_index_in_dim(a, source, 0, False), gathered)

    return lax.fori_loop(
        1, lax.axis_size(axis), lambda source, state: combine(state, take(source)), take(0)
    )


def combine_stats(first, second):
    upper = jnp.maximum(first[0], second[0])
    return (upper, first[1] * jnp.exp(first[0] - upper) + second[1] * jnp.exp(second[0] - upper))


def local(vectors, block_sides, centers):
    step_size = 2 ** (LEVEL + 1)
    cycle_len = lax.axis_size("wide") // step_size
    wide_place = lax.axis_index("wide")
    cycle_place = wide_place // step_size
    own_side = wide_place // 2**LEVEL % 2
    feat_width = vectors.shape[1]
    block_count = block_sides.shape[0]
    half_blocks = block_count // 2
    blocks = vectors.reshape(block_count, -1, feat_width)
    block_order = jnp.argsort(
        jnp.where(block_sides == own_side, 0, 1).astype(jnp.int32), stable=True
    )
    arranged = jnp.take(blocks, block_order, axis=0)
    incoming = from_partner(arranged[half_blocks:], "wide", LEVEL)
    local_rows = jnp.concatenate([arranged[:half_blocks], incoming], axis=0).reshape(-1, feat_width)
    gathered = lax.all_gather(local_rows, "narrow", axis=0, tiled=True)
    row_count = gathered.shape[0]
    shard_rows = centers.shape[0]
    score_scale = 4.0 / math.sqrt(feat_width)
    zero_index = jnp.zeros((), jnp.int32)

    def score_block(center):
        sq_norms = jnp.sum(center.astype(jnp.float32) ** 2, axis=1)
        products = lax.dot_general(
            gathered, center, (((1,), (1,)), ((), ())), preferred_element_type=jnp.float32
        )
        return score_scale * (products - 0.5 * sq_norms[None, :])

    def put_block(table, center, source):
        column = source % cycle_len * shard_rows
        return lax.dynamic_update_slice(table, score_block(center), (zero_index, column))

    def block_terms(weights, source, offset, length):
        column = source % cycle_len * shard_rows + offset
        columns = lax.dynamic_slice_in_dim(weights, column, length, 1)
        numerator = lax.dot_general(
            columns, gathered, (((0,), (0,)), ((), ())), preferred_element_type=jnp.float32
        )
        return (numerator, jnp.sum(columns.astype(jnp.float32), axis=0))

    for sweep_num in range(ITERS):
        scores = jnp.zeros((row_count, cycle_len * shard_rows), jnp.float32)
        scores = put_block(scores, centers, cycle_place)

        def stream_one(step_num, loop_state):
            current, table = loop_state
            current = shifted(current, "wide", step_size)
            return (current, put_block(table, current, cycle_place - step_num))

        current, scores = lax.fori_loop(1, cycle_len, stream_one, (centers, scores))
        row_top = jnp.max(scores, axis=1)
        row_sum = jnp.sum(jnp.exp(scores - row_top[:, None]), axis=1)
        full_top, full_sum = combined_all((row_top, row_sum), "narrow", combine_stats)
        weights = (jnp.exp(scores - full_top[:, None]) / full_sum[:, None]).astype(jnp.bfloat16)

        def gather_one(step_num, loop_state):
            moved = shifted((loop_state[0], loop_state[1]), "wide", step_size)
            added = block_terms(weights, cycle_place - step_num - 1, 0, shard_rows)
            return (moved[0] + added[0], moved[1] + added[1])

        numerator, denominator = lax.fori_loop(
            1, cycle_len, gather_one, block_terms(weights, cycle_place - 1, 0, shard_rows)
        )
        centers = ((numerator + centers.astype(jnp.float32)) / (denominator + 1.0)[:, None]).astype(
            jnp.bfloat16
        )
    return centers


def solution(mesh):
    in_specs = (P(("wide", "narrow"), None), P(("wide", "narrow")), P(("wide", "narrow"), None))
    out_specs = P(("wide", "narrow"), None)
    return jax.shard_map(local, mesh=mesh, in_specs=in_specs, out_specs=out_specs, check_vma=False)
```

profile of v0, /device:TPU:32, one launch (start us, length us, event | category | flops | bytes accessed | tf_op | source)
XLA Modules:
  0.0 849.5 jit_solution(4124487896540554424)
XLA Ops:
  18.0 68.8 %all-gather.6.cloned.1.call-done = bf16[2048,768]{1,0:T(8,128)(2,1)} async-done(((bf16[256,768]{1,0:T(8,128)(2,1)}), bf16[2048,768]{1,0:T(8,128)(2,1)}) %all-gather.6.cloned.1.call-update) | async-done | bytes 3145744 | tf_op jit(solution)/shard_map/all_gather | solution.py:56
  92.8 114.8 %while.102 = (s32[]{:T(128)}, bf16[128,768]{1,0:T(8,128)(2,1)}, f32[2048,1024]{1,0:T(8,128)}, bf16[2048,768]{1,0:T(8,128)(2,1)S(1)}, s32[]{:T(128)}, /*index=5*/...) while((s32[]{:T(128)}, bf16[128,768]{1,0:T(8,128)(2,1)}, ...), condition=%wide.region_4.5_spmd, body=%wide.region_2.4_spmd.sunk | while | flops 403472416 | bytes 5769536 | solution.py:90
  95.4 10.8 %collective-permute-done = bf16[128,768]{1,0:T(8,128)(2,1)} collective-permute-done((bf16[128,768]{1,0:T(8,128)(2,1)}, bf16[128,768]{1,0:T(8,128)(2,1)}, u32[]{:S(2)}, u32[]{:S(2)}) %collective-permute-start) | collective-permute-done | bytes 196640 | tf_op jit(solution)/shard_map/while/body/eval_jaxpr/ppermute | solution.py:21
  112.4 12.0 %collective-permute-done = bf16[128,768]{1,0:T(8,128)(2,1)} collective-permute-done((bf16[128,768]{1,0:T(8,128)(2,1)}, bf16[128,768]{1,0:T(8,128)(2,1)}, u32[]{:S(2)}, u32[]{:S(2)}) %collective-permute-start) | collective-permute-done | bytes 196640 | tf_op jit(solution)/shard_map/while/body/eval_jaxpr/ppermute | solution.py:21
  130.0 12.0 %collective-permute-done = bf16[128,768]{1,0:T(8,128)(2,1)} collective-permute-done((bf16[128,768]{1,0:T(8,128)(2,1)}, bf16[128,768]{1,0:T(8,128)(2,1)}, u32[]{:S(2)}, u32[]{:S(2)}) %collective-permute-start) | collective-permute-done | bytes 196640 | tf_op jit(solution)/shard_map/while/body/eval_jaxpr/ppermute | solution.py:21
  147.6 9.2 %collective-permute-done = bf16[128,768]{1,0:T(8,128)(2,1)} collective-permute-done((bf16[128,768]{1,0:T(8,128)(2,1)}, bf16[128,768]{1,0:T(8,128)(2,1)}, u32[]{:S(2)}, u32[]{:S(2)}) %collective-permute-start) | collective-permute-done | bytes 196640 | tf_op jit(solution)/shard_map/while/body/eval_jaxpr/ppermute | solution.py:21
  177.2 10.0 %collective-permute-done = bf16[128,768]{1,0:T(8,128)(2,1)} collective-permute-done((bf16[128,768]{1,0:T(8,128)(2,1)}, bf16[128,768]{1,0:T(8,128)(2,1)}, u32[]{:S(2)}, u32[]{:S(2)}) %collective-permute-start) | collective-permute-done | bytes 196640 | tf_op jit(solution)/shard_map/while/body/eval_jaxpr/ppermute | solution.py:21
  215.8 36.2 %all-gather.1 = f32[16384]{0:T(1024)} all-gather(f32[2048]{0:T(1024)S(1)} %exponential_reduce_fusion.1), channel_id=3, replica_groups=mesh['wide'=32,'narrow'=8] {'narrow'}, dimensions={0}, use_global_device_ids=true | all-gather | bytes 73728 | tf_op jit(solution)/shard_map/all_gather | solution.py:25
  254.2 36.3 %all-gather = f32[16384]{0:T(1024)} all-gather(f32[2048]{0:T(1024)S(1)} %reduce_max.18), channel_id=2, replica_groups=mesh['wide'=32,'narrow'=8] {'narrow'}, dimensions={0}, use_global_device_ids=true | all-gather | bytes 73728 | tf_op jit(solution)/shard_map/all_gather | solution.py:25
  305.5 155.7 %while.104 = (s32[]{:T(128)}, f32[128,768]{1,0:T(8,128)}, f32[128]{0:T(128)S(1)}, s32[]{:T(128)}, bf16[2048,1024]{1,0:T(8,128)(2,1)}, /*index=5*/bf16[2048,768]{...) while((s32[]{:T(128)}, f32[128,768]{1,0:T(8,128)}, ...), condition=%wide.region_12.13_spmd, body=%wide.region_10.12_spmd.sunk | while | flops 403275808 | bytes 6558088 | solution.py:101
  313.0 12.6 %collective-permute-done.2 = f32[128]{0:T(128)S(1)} collective-permute-done((f32[128]{0:T(128)S(1)}, f32[128]{0:T(128)S(1)}, u32[]{:S(2)}, u32[]{:S(2)}) %collective-permute-start.2) | collective-permute-done | bytes 544 | tf_op jit(solution)/shard_map/while/body/eval_jaxpr/ppermute | solution.py:21
  404.2 12.3 %collective-permute-done.2 = f32[128]{0:T(128)S(1)} collective-permute-done((f32[128]{0:T(128)S(1)}, f32[128]{0:T(128)S(1)}, u32[]{:S(2)}, u32[]{:S(2)}) %collective-permute-start.2) | collective-permute-done | bytes 544 | tf_op jit(solution)/shard_map/while/body/eval_jaxpr/ppermute | solution.py:21
  425.5 13.0 %collective-permute-done.2 = f32[128]{0:T(128)S(1)} collective-permute-done((f32[128]{0:T(128)S(1)}, f32[128]{0:T(128)S(1)}, u32[]{:S(2)}, u32[]{:S(2)}) %collective-permute-start.2) | collective-permute-done | bytes 544 | tf_op jit(solution)/shard_map/while/body/eval_jaxpr/ppermute | solution.py:21
  468.4 115.8 %while.105 = (s32[]{:T(128)}, bf16[128,768]{1,0:T(8,128)(2,1)}, f32[2048,1024]{1,0:T(8,128)}, bf16[2048,768]{1,0:T(8,128)(2,1)S(1)}, s32[]{:T(128)}, /*index=5*/...) while((s32[]{:T(128)}, bf16[128,768]{1,0:T(8,128)(2,1)}, ...), condition=%wide.region_16.17_spmd, body=%wide.region_14.16_spmd.sunk | while | flops 403472416 | bytes 5769536 | solution.py:90
  592.5 46.8 %all-gather.3 = f32[16384]{0:T(1024)} all-gather(f32[2048]{0:T(1024)S(1)} %exponential_reduce_fusion), channel_id=5, replica_groups=mesh['wide'=32,'narrow'=8] {'narrow'}, dimensions={0}, use_global_device_ids=true | all-gather | bytes 73728 | tf_op jit(solution)/shard_map/all_gather | solution.py:25
  641.5 36.4 %all-gather.2 = f32[16384]{0:T(1024)} all-gather(f32[2048]{0:T(1024)S(1)} %reduce_max.19), channel_id=4, replica_groups=mesh['wide'=32,'narrow'=8] {'narrow'}, dimensions={0}, use_global_device_ids=true | all-gather | bytes 73728 | tf_op jit(solution)/shard_map/all_gather | solution.py:25
  692.9 147.9 %while.107 = (s32[]{:T(128)}, f32[128,768]{1,0:T(8,128)}, f32[128]{0:T(128)S(1)}, s32[]{:T(128)}, bf16[2048,1024]{1,0:T(8,128)(2,1)}, /*index=5*/bf16[2048,768]{...) while((s32[]{:T(128)}, f32[128,768]{1,0:T(8,128)}, ...), condition=%wide.region_24.25_spmd, body=%wide.region_22.24_spmd.sunk | while | flops 403275808 | bytes 6558088 | solution.py:101
  702.8 13.7 %collective-permute-done.5 = f32[128]{0:T(128)S(1)} collective-permute-done((f32[128]{0:T(128)S(1)}, f32[128]{0:T(128)S(1)}, u32[]{:S(2)}, u32[]{:S(2)}) %collective-permute-start.5) | collective-permute-done | bytes 544 | tf_op jit(solution)/shard_map/while/body/eval_jaxpr/ppermute | solution.py:21
  720.4 19.4 %collective-permute-done.5 = f32[128]{0:T(128)S(1)} collective-permute-done((f32[128]{0:T(128)S(1)}, f32[128]{0:T(128)S(1)}, u32[]{:S(2)}, u32[]{:S(2)}) %collective-permute-start.5) | collective-permute-done | bytes 544 | tf_op jit(solution)/shard_map/while/body/eval_jaxpr/ppermute | solution.py:21
  743.7 21.9 %collective-permute-done.5 = f32[128]{0:T(128)S(1)} collective-permute-done((f32[128]{0:T(128)S(1)}, f32[128]{0:T(128)S(1)}, u32[]{:S(2)}, u32[]{:S(2)}) %collective-permute-start.5) | collective-permute-done | bytes 544 | tf_op jit(solution)/shard_map/while/body/eval_jaxpr/ppermute | solution.py:21
  769.6 18.2 %collective-permute-done.5 = f32[128]{0:T(128)S(1)} collective-permute-done((f32[128]{0:T(128)S(1)}, f32[128]{0:T(128)S(1)}, u32[]{:S(2)}, u32[]{:S(2)}) %collective-permute-start.5) | collective-permute-done | bytes 544 | tf_op jit(solution)/shard_map/while/body/eval_jaxpr/ppermute | solution.py:21
  791.7 11.0 %collective-permute-done.5 = f32[128]{0:T(128)S(1)} collective-permute-done((f32[128]{0:T(128)S(1)}, f32[128]{0:T(128)S(1)}, u32[]{:S(2)}, u32[]{:S(2)}) %collective-permute-start.5) | collective-permute-done | bytes 544 | tf_op jit(solution)/shard_map/while/body/eval_jaxpr/ppermute | solution.py:21
  806.5 14.0 %collective-permute-done.5 = f32[128]{0:T(128)S(1)} collective-permute-done((f32[128]{0:T(128)S(1)}, f32[128]{0:T(128)S(1)}, u32[]{:S(2)}, u32[]{:S(2)}) %collective-permute-start.5) | collective-permute-done | bytes 544 | tf_op jit(solution)/shard_map/while/body/eval_jaxpr/ppermute | solution.py:21
  824.3 13.9 %collective-permute-done.5 = f32[128]{0:T(128)S(1)} collective-permute-done((f32[128]{0:T(128)S(1)}, f32[128]{0:T(128)S(1)}, u32[]{:S(2)}, u32[]{:S(2)}) %collective-permute-start.5) | collective-permute-done | bytes 544 | tf_op jit(solution)/shard_map/while/body/eval_jaxpr/ppermute | solution.py:21
  (260 shorter events, 420.0 us)
Async XLA Ops:
  6.5 80.2 %all-gather.6.cloned.1.call-start = ((), (), s32[]{:S(2)}) async-start(), calls=%async_computation | async-start | bytes 3538944 | tf_op jit(solution)/shard_map/all_gather | solution.py:56
  305.5 20.1 %collective-permute-start.1 = (f32[128,768]{1,0:T(8,128)}, f32[128,768]{1,0:T(8,128)}, u32[]{:S(2)}, u32[]{:S(2)}) collective-permute-start(f32[128,768]{1,0:T(8,128)} %get-tuple-element.1224), channel_id=1, source_target_pairs={{0,32},{8,40},{16,48},{24,56},{32,64},{40,72},{48,80},{56,88},{64,... | collective-permute-start | bytes 1179656 | tf_op jit(solution)/shard_map/while/body/eval_jaxpr/ppermute | solution.py:21
  307.0 18.6 %collective-permute-start.2 = (f32[128]{0:T(128)S(1)}, f32[128]{0:T(128)S(1)}, u32[]{:S(2)}, u32[]{:S(2)}) collective-permute-start(f32[128]{0:T(128)S(1)} %get-tuple-element.1225), channel_id=1, source_target_pairs={{0,32},{8,40},{16,48},{24,56},{32,64},{40,72},{48,80},{56,88},{64,... | collective-permute-start | bytes 1544 | tf_op jit(solution)/shard_map/while/body/eval_jaxpr/ppermute | solution.py:21
  328.1 20.3 %collective-permute-start.1 = (f32[128,768]{1,0:T(8,128)}, f32[128,768]{1,0:T(8,128)}, u32[]{:S(2)}, u32[]{:S(2)}) collective-permute-start(f32[128,768]{1,0:T(8,128)} %get-tuple-element.1224), channel_id=1, source_target_pairs={{0,32},{8,40},{16,48},{24,56},{32,64},{40,72},{48,80},{56,88},{64,... | collective-permute-start | bytes 1179656 | tf_op jit(solution)/shard_map/while/body/eval_jaxpr/ppermute | solution.py:21
  330.7 17.8 %collective-permute-start.2 = (f32[128]{0:T(128)S(1)}, f32[128]{0:T(128)S(1)}, u32[]{:S(2)}, u32[]{:S(2)}) collective-permute-start(f32[128]{0:T(128)S(1)} %get-tuple-element.1225), channel_id=1, source_target_pairs={{0,32},{8,40},{16,48},{24,56},{32,64},{40,72},{48,80},{56,88},{64,... | collective-permute-start | bytes 1544 | tf_op jit(solution)/shard_map/while/body/eval_jaxpr/ppermute | solution.py:21
  351.0 22.1 %collective-permute-start.1 = (f32[128,768]{1,0:T(8,128)}, f32[128,768]{1,0:T(8,128)}, u32[]{:S(2)}, u32[]{:S(2)}) collective-permute-start(f32[128,768]{1,0:T(8,128)} %get-tuple-element.1224), channel_id=1, source_target_pairs={{0,32},{8,40},{16,48},{24,56},{32,64},{40,72},{48,80},{56,88},{64,... | collective-permute-start | bytes 1179656 | tf_op jit(solution)/shard_map/while/body/eval_jaxpr/ppermute | solution.py:21
  375.6 18.0 %collective-permute-start.1 = (f32[128,768]{1,0:T(8,128)}, f32[128,768]{1,0:T(8,128)}, u32[]{:S(2)}, u32[]{:S(2)}) collective-permute-start(f32[128,768]{1,0:T(8,128)} %get-tuple-element.1224), channel_id=1, source_target_pairs={{0,32},{8,40},{16,48},{24,56},{32,64},{40,72},{48,80},{56,88},{64,... | collective-permute-start | bytes 1179656 | tf_op jit(solution)/shard_map/while/body/eval_jaxpr/ppermute | solution.py:21
  396.2 20.4 %collective-permute-start.1 = (f32[128,768]{1,0:T(8,128)}, f32[128,768]{1,0:T(8,128)}, u32[]{:S(2)}, u32[]{:S(2)}) collective-permute-start(f32[128,768]{1,0:T(8,128)} %get-tuple-element.1224), channel_id=1, source_target_pairs={{0,32},{8,40},{16,48},{24,56},{32,64},{40,72},{48,80},{56,88},{64,... | collective-permute-start | bytes 1179656 | tf_op jit(solution)/shard_map/while/body/eval_jaxpr/ppermute | solution.py:21
  399.6 16.9 %collective-permute-start.2 = (f32[128]{0:T(128)S(1)}, f32[128]{0:T(128)S(1)}, u32[]{:S(2)}, u32[]{:S(2)}) collective-permute-start(f32[128]{0:T(128)S(1)} %get-tuple-element.1225), channel_id=1, source_target_pairs={{0,32},{8,40},{16,48},{24,56},{32,64},{40,72},{48,80},{56,88},{64,... | collective-permute-start | bytes 1544 | tf_op jit(solution)/shard_map/while/body/eval_jaxpr/ppermute | solution.py:21
  419.1 19.5 %collective-permute-start.1 = (f32[128,768]{1,0:T(8,128)}, f32[128,768]{1,0:T(8,128)}, u32[]{:S(2)}, u32[]{:S(2)}) collective-permute-start(f32[128,768]{1,0:T(8,128)} %get-tuple-element.1224), channel_id=1, source_target_pairs={{0,32},{8,40},{16,48},{24,56},{32,64},{40,72},{48,80},{56,88},{64,... | collective-permute-start | bytes 1179656 | tf_op jit(solution)/shard_map/while/body/eval_jaxpr/ppermute | solution.py:21
  422.4 16.1 %collective-permute-start.2 = (f32[128]{0:T(128)S(1)}, f32[128]{0:T(128)S(1)}, u32[]{:S(2)}, u32[]{:S(2)}) collective-permute-start(f32[128]{0:T(128)S(1)} %get-tuple-element.1225), channel_id=1, source_target_pairs={{0,32},{8,40},{16,48},{24,56},{32,64},{40,72},{48,80},{56,88},{64,... | collective-permute-start | bytes 1544 | tf_op jit(solution)/shard_map/while/body/eval_jaxpr/ppermute | solution.py:21
  441.1 17.5 %collective-permute-start.1 = (f32[128,768]{1,0:T(8,128)}, f32[128,768]{1,0:T(8,128)}, u32[]{:S(2)}, u32[]{:S(2)}) collective-permute-start(f32[128,768]{1,0:T(8,128)} %get-tuple-element.1224), channel_id=1, source_target_pairs={{0,32},{8,40},{16,48},{24,56},{32,64},{40,72},{48,80},{56,88},{64,... | collective-permute-start | bytes 1179656 | tf_op jit(solution)/shard_map/while/body/eval_jaxpr/ppermute | solution.py:21
  692.9 23.7 %collective-permute-start.4 = (f32[128,768]{1,0:T(8,128)}, f32[128,768]{1,0:T(8,128)}, u32[]{:S(2)}, u32[]{:S(2)}) collective-permute-start(f32[128,768]{1,0:T(8,128)} %get-tuple-element.1320), channel_id=1, source_target_pairs={{0,32},{8,40},{16,48},{24,56},{32,64},{40,72},{48,80},{56,88},{64,... | collective-permute-start | bytes 1179656 | tf_op jit(solution)/shard_map/while/body/eval_jaxpr/ppermute | solution.py:21
  696.9 19.6 %collective-permute-start.5 = (f32[128]{0:T(128)S(1)}, f32[128]{0:T(128)S(1)}, u32[]{:S(2)}, u32[]{:S(2)}) collective-permute-start(f32[128]{0:T(128)S(1)} %get-tuple-element.1321), channel_id=1, source_target_pairs={{0,32},{8,40},{16,48},{24,56},{32,64},{40,72},{48,80},{56,88},{64,... | collective-permute-start | bytes 1544 | tf_op jit(solution)/shard_map/while/body/eval_jaxpr/ppermute | solution.py:21
  719.1 20.8 %collective-permute-start.4 = (f32[128,768]{1,0:T(8,128)}, f32[128,768]{1,0:T(8,128)}, u32[]{:S(2)}, u32[]{:S(2)}) collective-permute-start(f32[128,768]{1,0:T(8,128)} %get-tuple-element.1320), channel_id=1, source_target_pairs={{0,32},{8,40},{16,48},{24,56},{32,64},{40,72},{48,80},{56,88},{64,... | collective-permute-start | bytes 1179656 | tf_op jit(solution)/shard_map/while/body/eval_jaxpr/ppermute | solution.py:21
  719.1 20.8 %collective-permute-start.5 = (f32[128]{0:T(128)S(1)}, f32[128]{0:T(128)S(1)}, u32[]{:S(2)}, u32[]{:S(2)}) collective-permute-start(f32[128]{0:T(128)S(1)} %get-tuple-element.1321), channel_id=1, source_target_pairs={{0,32},{8,40},{16,48},{24,56},{32,64},{40,72},{48,80},{56,88},{64,... | collective-permute-start | bytes 1544 | tf_op jit(solution)/shard_map/while/body/eval_jaxpr/ppermute | solution.py:21
  742.4 23.3 %collective-permute-start.4 = (f32[128,768]{1,0:T(8,128)}, f32[128,768]{1,0:T(8,128)}, u32[]{:S(2)}, u32[]{:S(2)}) collective-permute-start(f32[128,768]{1,0:T(8,128)} %get-tuple-element.1320), channel_id=1, source_target_pairs={{0,32},{8,40},{16,48},{24,56},{32,64},{40,72},{48,80},{56,88},{64,... | collective-permute-start | bytes 1179656 | tf_op jit(solution)/shard_map/while/body/eval_jaxpr/ppermute | solution.py:21
  742.4 23.3 %collective-permute-start.5 = (f32[128]{0:T(128)S(1)}, f32[128]{0:T(128)S(1)}, u32[]{:S(2)}, u32[]{:S(2)}) collective-permute-start(f32[128]{0:T(128)S(1)} %get-tuple-element.1321), channel_id=1, source_target_pairs={{0,32},{8,40},{16,48},{24,56},{32,64},{40,72},{48,80},{56,88},{64,... | collective-permute-start | bytes 1544 | tf_op jit(solution)/shard_map/while/body/eval_jaxpr/ppermute | solution.py:21
  768.2 19.6 %collective-permute-start.4 = (f32[128,768]{1,0:T(8,128)}, f32[128,768]{1,0:T(8,128)}, u32[]{:S(2)}, u32[]{:S(2)}) collective-permute-start(f32[128,768]{1,0:T(8,128)} %get-tuple-element.1320), channel_id=1, source_target_pairs={{0,32},{8,40},{16,48},{24,56},{32,64},{40,72},{48,80},{56,88},{64,... | collective-permute-start | bytes 1179656 | tf_op jit(solution)/shard_map/while/body/eval_jaxpr/ppermute | solution.py:21
  768.2 19.5 %collective-permute-start.5 = (f32[128]{0:T(128)S(1)}, f32[128]{0:T(128)S(1)}, u32[]{:S(2)}, u32[]{:S(2)}) collective-permute-start(f32[128]{0:T(128)S(1)} %get-tuple-element.1321), channel_id=1, source_target_pairs={{0,32},{8,40},{16,48},{24,56},{32,64},{40,72},{48,80},{56,88},{64,... | collective-permute-start | bytes 1544 | tf_op jit(solution)/shard_map/while/body/eval_jaxpr/ppermute | solution.py:21
  805.2 15.3 %collective-permute-start.4 = (f32[128,768]{1,0:T(8,128)}, f32[128,768]{1,0:T(8,128)}, u32[]{:S(2)}, u32[]{:S(2)}) collective-permute-start(f32[128,768]{1,0:T(8,128)} %get-tuple-element.1320), channel_id=1, source_target_pairs={{0,32},{8,40},{16,48},{24,56},{32,64},{40,72},{48,80},{56,88},{64,... | collective-permute-start | bytes 1179656 | tf_op jit(solution)/shard_map/while/body/eval_jaxpr/ppermute | solution.py:21
  805.2 15.3 %collective-permute-start.5 = (f32[128]{0:T(128)S(1)}, f32[128]{0:T(128)S(1)}, u32[]{:S(2)}, u32[]{:S(2)}) collective-permute-start(f32[128]{0:T(128)S(1)} %get-tuple-element.1321), channel_id=1, source_target_pairs={{0,32},{8,40},{16,48},{24,56},{32,64},{40,72},{48,80},{56,88},{64,... | collective-permute-start | bytes 1544 | tf_op jit(solution)/shard_map/while/body/eval_jaxpr/ppermute | solution.py:21
  823.0 15.2 %collective-permute-start.4 = (f32[128,768]{1,0:T(8,128)}, f32[128,768]{1,0:T(8,128)}, u32[]{:S(2)}, u32[]{:S(2)}) collective-permute-start(f32[128,768]{1,0:T(8,128)} %get-tuple-element.1320), channel_id=1, source_target_pairs={{0,32},{8,40},{16,48},{24,56},{32,64},{40,72},{48,80},{56,88},{64,... | collective-permute-start | bytes 1179656 | tf_op jit(solution)/shard_map/while/body/eval_jaxpr/ppermute | solution.py:21
  823.0 15.2 %collective-permute-start.5 = (f32[128]{0:T(128)S(1)}, f32[128]{0:T(128)S(1)}, u32[]{:S(2)}, u32[]{:S(2)}) collective-permute-start(f32[128]{0:T(128)S(1)} %get-tuple-element.1321), channel_id=1, source_target_pairs={{0,32},{8,40},{16,48},{24,56},{32,64},{40,72},{48,80},{56,88},{64,... | collective-permute-start | bytes 1544 | tf_op jit(solution)/shard_map/while/body/eval_jaxpr/ppermute | solution.py:21
  (29 other events, 254.7 us)
Sparse Core Ops, SparseCore 0:
  16.3 70.3 all-gather.5
where the time goes:
time: 853 us; the launch traced here: 849 us
  waiting for transfers between devices  368 us (43%)
  blocking collectives  156 us (18%)
  starting transfers between devices  109 us (13%)
  matrix products  82.4 us (10%)
  other arithmetic  64.4 us (8%)
  local copies, waits for them, and re-layouts  56.2 us (7%)
  between operations  13.6 us (2%)
    ppermute x42, waiting for transfers between devices, shifted(): return lax.ppermute(value, axis, pairs)  294 us
    all_gather x4, blocking collectives, combined_all(): gathered = jax.tree.map(lambda a: lax.all_gather(a, axis), part)  156 us
    ppermute x42, starting transfers between devices, shifted(): return lax.ppermute(value, axis, pairs)  107 us
    all_gather x1, waiting for transfers between devices, local(): gathered = lax.all_gather(local_rows, 'narrow', axis=0, tiled=True)  68.8 us
    dot_general x16, matrix products, score_block(): lax.dot_general(gathered, center, (((1,), (1,)), ((), ())), preferred_ele...  43.2 us
    dot_general x16, matrix products, block_terms(): lax.dot_general(columns, gathered, (((0,), (0,)), ((), ())), preferred_el...  39.2 us
    while x14, local copies, waits for them, and re-layouts  22.6 us
    reduce_sum x16, other arithmetic, block_terms(): return (numerator, jnp.sum(columns.astype(jnp.float32), axis=0))  19.1 us
  transfers between devices with their start and end apart: 44, of which 30 were waited for; matrix products, arithmetic and copies ran while one was open for 2% of the time, Pallas kernels for 0%

commit v1 on v0

v1 whole, which is shorter than its diff:
```python
import functools
import heapq
import math

import jax
import jax.numpy as jnp
from jax import lax
from jax.experimental import pallas as pl
from jax.experimental.pallas import tpu as pltpu
from jax.sharding import PartitionSpec as P

MESH = pl.DeviceIdType.MESH
D = 768
KS = 128
PIECE = 64
PIECES = 4
ROWS = PIECE * PIECES
SRC = 16
CHUNK = ROWS
ITERS = 2
Y_FIRST = (3,)
SCALE = 4.0 / math.sqrt(D) * math.log2(math.e)
F32 = jnp.float32
NT = (((1,), (1,)), ((), ()))


def hops(p, f, s):
    out = []
    if s == 0:
        relay = 1 if p % 2 == 0 else -1
        if f == 0:
            out += [("f", 1), ("f", -1)]
        elif (f == 1 and relay == 1) or (f == 3 and relay == -1):
            out.append(("f", relay))
        out += [("s", 1), ("s", -1)]
    else:
        relay = 1 if (p + f) % 2 == 0 else -1
        if (s == 1 and relay == 1) or (s == 3 and relay == -1):
            out.append(("s", relay))
    return out


def sends(key):
    p, dy, dz = key
    y_first = p in Y_FIRST
    f, s = (dy, dz) if y_first else (dz, dy)
    res = []
    for dim, step in hops(p, f, s):
        nf, ns = ((f + step) % 4, s) if dim == "f" else (f, (s + step) % 4)
        axis = ("y" if dim == "f" else "z") if y_first else ("z" if dim == "f" else "y")
        res.append((axis, step, (p, nf, ns) if y_first else (p, ns, nf)))
    return res


def plan():
    cost = {"y": 2.1, "z": 4.2}
    lat = {"y": 1.7, "z": 2.4}
    free = {}
    heap = [(0.0, 0, (0, 0, 0)), (0.0, 1, (1, 0, 0)), (5.0, 2, (2, 0, 0)), (7.0, 3, (3, 0, 0))]
    count = 4
    order = []
    while heap:
        now, unused, key = heapq.heappop(heap)
        order.append(key)
        for axis, step, target in sends(key):
            link = (axis, step)
            start = max(now, free.get(link, 0.0))
            free[link] = start + cost[axis]
            heapq.heappush(heap, (free[link] + lat[axis], count, target))
            count += 1
    return order, max(free.values())


def sem_of(key):
    p, dy, dz = key
    return p * 16 + dy * 4 + dz


def kernel(
    vec_ref, sides_ref, cen_ref, out_ref,
    x_all, swap_out, cen, hn, e_all, m_all, l_all, f_one, den_acc, lse_all, num, relay_in, main_in, den_out, den_in,
    x_send, x_recv, c_send, c_recv, l_send, l_recv, n_send, n_recv, d_send, d_recv,
):
    wide = lax.axis_index("wide")
    narrow = lax.axis_index("narrow")
    core = lax.rem(wide, 2)
    z = lax.rem(wide // 2, 8)
    y = lax.rem(narrow // 4, 2) * 2 + wide // 16
    x = lax.rem(narrow, 4)
    zp = z // 2
    parity = lax.rem(z, 2)
    me = y * 4 + zp

    def device(dx, ny, nz):
        nx = lax.rem(x + dx + 4, 4)
        return (lax.rem(ny, 2) * 16 + nz * 2 + core, (ny // 2) * 4 + nx)

    def plane(dy, dz):
        return device(0, lax.rem(y + dy + 4, 4), lax.rem(z + 2 * dz + 8, 8))

    def peer(index):
        return device(0, index // 4, lax.rem(index, 4) * 2 + parity)

    def across(dx):
        return device(dx, y, z)

    partner = device(0, y, z + 1 - 2 * parity)

    first = vec_ref[0:KS, :]
    second = vec_ref[KS : 2 * KS, :]
    first_stays = sides_ref[0] == parity
    base = pl.multiple_of(me * ROWS, ROWS)
    x_all[pl.ds(base, KS), :] = jnp.where(first_stays, first, second)
    swap_out[...] = jnp.where(first_stays, second, first)

    barrier = pltpu.get_barrier_semaphore()

    def greet(k, carry):
        pl.semaphore_signal(barrier, inc=1, device_id=peer(lax.rem(me + k, SRC)), device_id_type=MESH)
        return carry

    lax.fori_loop(1, SRC, greet, 0)
    for other in (partner, across(1), across(-1), across(2)):
        pl.semaphore_signal(barrier, inc=1, device_id=other, device_id_type=MESH)
    pl.semaphore_wait(barrier, SRC + 3)

    started = []

    def send(src, dst, send_sem, recv_sem, to):
        copy = pltpu.make_async_remote_copy(
            src_ref=src, dst_ref=dst, send_sem=send_sem, recv_sem=recv_sem, device_id=to, device_id_type=MESH
        )
        copy.start()
        started.append(copy)

    def arrived(dst, sem):
        pltpu.make_async_remote_copy(
            src_ref=dst, dst_ref=dst, send_sem=sem, recv_sem=sem, device_id=partner, device_id_type=MESH
        ).wait_recv()

    def piece(source, p):
        return x_all.at[pl.ds(pl.multiple_of(source * ROWS + p * PIECE, PIECE), PIECE), :]

    def source_of(dy, dz):
        return lax.rem(y - dy + 4, 4) * 4 + lax.rem(zp - dz + 4, 4)

    for half in (0, 1):
        send(
            swap_out.at[pl.ds(half * PIECE, PIECE), :], piece(me, 2 + half),
            x_send.at[sem_of((2 + half, 0, 0))], x_recv.at[sem_of((2 + half, 0, 0))], partner,
        )

    def send_centers(it, own):
        for step, slot in ((1, 1), (-1, 2)):
            for half in (0, 1) if step == 1 else (1, 0):
                rows = pl.ds(half * 64, 64)
                index = it * 6 + (slot - 1) * 2 + half
                send(
                    own.at[rows, :], cen.at[it, pl.ds(slot * KS + half * 64, 64), :],
                    c_send.at[index], c_recv.at[index], across(step),
                )

    def relay_centers(it):
        for step, slot, half in ((1, 1, 0), (-1, 2, 1)):
            rows = pl.ds(slot * KS + half * 64, 64)
            arrived(cen.at[it, rows, :], c_recv.at[it * 6 + (slot - 1) * 2 + half])
            index = it * 6 + 4 + half
            send(
                cen.at[it, rows, :], cen.at[it, pl.ds(3 * KS + half * 64, 64), :],
                c_send.at[index], c_recv.at[index], across(step),
            )

    def norms(it, q):
        c = cen[it, pl.ds(q * KS, KS), :].astype(F32)
        n = 0.5 * jnp.sum(c * c, axis=1, keepdims=True)
        hn[q] = jnp.broadcast_to(n, (KS, 128))

    def exponents(q, r, product):
        half = hn[q]
        s = (product - jnp.concatenate([half, half], axis=1)) * SCALE
        top = jnp.max(s, axis=0, keepdims=True)
        e = jnp.exp2(s - top)
        e_all[q, r] = e
        m_all[q, pl.ds(r, 1), :] = top
        l_all[q, pl.ds(r, 1), :] = jnp.sum(e, axis=0, keepdims=True)

    def scores(it, q, r):
        rows = x_all[pl.ds(pl.multiple_of(r * CHUNK, CHUNK), CHUNK), :]
        product = lax.dot_general(
            cen[it, pl.ds(q * KS, KS), :], rows, NT, preferred_element_type=F32
        )
        exponents(q, r, product)

    def score_chunk(r):
        rows = x_all[pl.ds(pl.multiple_of(r * CHUNK, CHUNK), CHUNK), :]
        for q in range(4):
            product = lax.dot_general(cen[0, pl.ds(q * KS, KS), :], rows, NT, preferred_element_type=F32)
            exponents(q, r, product)

    def score_block(it, q):
        norms(it, q)

        def one(r, carry):
            scores(it, q, r)
            return carry

        lax.fori_loop(0, SRC, one, 0)

    def exchange_lse(it):
        top = jnp.maximum(jnp.maximum(m_all[0], m_all[1]), jnp.maximum(m_all[2], m_all[3]))
        total = sum(l_all[q] * jnp.exp2(m_all[q] - top) for q in range(4))
        lse_all[it, me] = top + jnp.log2(total)

        def tell(k, carry):
            pltpu.make_async_remote_copy(
                src_ref=lse_all.at[it, me], dst_ref=lse_all.at[it, me],
                send_sem=l_send.at[it, k], recv_sem=l_recv.at[it, me],
                device_id=peer(lax.rem(me + k, SRC)), device_id_type=MESH,
            ).start()
            return carry

        lax.fori_loop(1, SRC, tell, 0)

        def hear(k, carry):
            other = lax.rem(me + k, SRC)
            arrived(lse_all.at[it, other], l_recv.at[it, other])
            return carry

        lax.fori_loop(1, SRC, hear, 0)
        best = lse_all[it, 0]
        for k in range(1, SRC):
            best = jnp.maximum(best, lse_all[it, k])
        total = jnp.exp2(lse_all[it, 0] - best)
        for k in range(1, SRC):
            total = total + jnp.exp2(lse_all[it, k] - best)
        return best + jnp.log2(total)

    def weigh(it, q, lse):
        f_one[q] = jnp.exp2(m_all[q] - lse)

        def group(g):
            parts = []
            den = jnp.zeros((KS, 128), F32)
            for j in range(4):
                r = g * 4 + j
                weights = (e_all[q, r] * f_one[q, pl.ds(r, 1), :]).astype(jnp.bfloat16)
                wide_weights = weights.astype(F32)
                den = den + wide_weights[:, :128] + wide_weights[:, 128:]
                parts.append(weights)
            rows = x_all[pl.ds(pl.multiple_of(g * 4 * CHUNK, 4 * CHUNK), 4 * CHUNK), :]
            term = jnp.dot(jnp.concatenate(parts, axis=1), rows, preferred_element_type=F32)
            return term, den

        num[it, q], den_acc[...] = group(0)

        def one(g, carry):
            term, den = group(g)
            num[it, q] += term
            den_acc[...] += den
            return carry

        lax.fori_loop(1, 4, one, 0)
        column = jnp.sum(den_acc[...], axis=1, keepdims=True)
        here = lax.broadcasted_iota(jnp.int32, (KS, 128), 0) == lax.broadcasted_iota(jnp.int32, (KS, 128), 1)
        row = jnp.sum(jnp.where(here, column, 0.0), axis=0, keepdims=True)
        den_out[it, q] = jnp.broadcast_to(row, (8, 128))

    def reduce_centers(it, lse, old):
        weigh(it, 3, lse)
        base = it * 6
        for i, (half, step) in enumerate(((0, 1), (1, -1))):
            send(
                num.at[it, 3, pl.ds(half * 64, 64), :], relay_in.at[it, i],
                n_send.at[base + i], n_recv.at[base + i], across(step),
            )
        send(den_out.at[it, 3], den_in.at[it, 3], d_send.at[it * 4 + 3], d_recv.at[it * 4 + 3], across(2))
        for i, (q, step, half) in enumerate(((2, 1, 1), (1, -1, 0))):
            weigh(it, q, lse)
            send(
                num.at[it, q, pl.ds(half * 64, 64), :], main_in.at[it, i, pl.ds(half * 64, 64), :],
                n_send.at[base + 2 + i], n_recv.at[base + 2 + i], across(step),
            )
            send(den_out.at[it, q], den_in.at[it, 3 - q], d_send.at[it * 4 + q], d_recv.at[it * 4 + 3 - q], across(step))
        for i, (q, step, half) in enumerate(((2, 1, 0), (1, -1, 1))):
            rows = pl.ds(half * 64, 64)
            arrived(relay_in.at[it, i], n_recv.at[base + i])
            num[it, q, rows, :] += relay_in[it, i]
            send(
                num.at[it, q, rows, :], main_in.at[it, i, rows, :],
                n_send.at[base + 4 + i], n_recv.at[base + 4 + i], across(step),
            )
        weigh(it, 0, lse)
        for i, half in enumerate((1, 0)):
            rows = pl.ds(half * 64, 64)
            arrived(main_in.at[it, i, rows, :], n_recv.at[base + 2 + i])
        for k in (1, 2, 3):
            arrived(den_in.at[it, k], d_recv.at[it * 4 + k])
        row = den_out[it, 0] + den_in[it, 1] + den_in[it, 2] + den_in[it, 3]
        here = lax.broadcasted_iota(jnp.int32, (KS, 128), 0) == lax.broadcasted_iota(jnp.int32, (KS, 128), 1)
        column = jnp.sum(jnp.where(here, row[0:1, :], 0.0), axis=1, keepdims=True)
        for i, half in enumerate((0, 1)):
            rows = pl.ds(half * 64, 64)
            arrived(main_in.at[it, i, rows, :], n_recv.at[base + 4 + i])
        total = num[it, 0] + main_in[it, 0] + main_in[it, 1]
        return ((total + old[...].astype(F32)) / (column + 1.0)).astype(jnp.bfloat16)

    order, unused = plan()
    seen = {}
    send_centers(0, cen_ref)
    cen[0, 0:KS, :] = cen_ref[...]
    norms(0, 0)
    ready = []
    centers_in = False
    for number, key in enumerate(order):
        p, dy, dz = key
        source = source_of(dy, dz)
        if key not in ((0, 0, 0), (1, 0, 0)):
            arrived(piece(source, p), x_recv.at[sem_of(key)])
        for axis, step, target in sends(key):
            to = plane(step, 0) if axis == "y" else plane(0, step)
            index = len([c for c in started if c is not None])
            send(piece(source, p), piece(source, p), x_send.at[64 + index - 6], x_recv.at[sem_of(target)], to)
        seen[(dy, dz)] = seen.get((dy, dz), 0) + 1
        if seen[(dy, dz)] == PIECES:
            ready.append(source)
        if number == 3:
            relay_centers(0)
        if number >= 12 and not centers_in:
            for index in (1, 2, 4, 5):
                slot, half = ((index // 2) + 1, index % 2) if index < 4 else (3, index - 4)
                arrived(cen.at[0, pl.ds(slot * KS + half * 64, 64), :], c_recv.at[index])
            for q in (1, 2, 3):
                norms(0, q)
            centers_in = True
        if centers_in:
            for r in ready:
                score_chunk(r)
            ready = []
    lse = exchange_lse(0)
    fresh = reduce_centers(0, lse, cen_ref)

    cen[1, 0:KS, :] = fresh
    own = cen.at[1, pl.ds(0, KS), :]
    send_centers(1, own)
    score_block(1, 0)
    relay_centers(1)
    for slot in (1, 2):
        half = 2 - slot
        arrived(cen.at[1, pl.ds(slot * KS + half * 64, 64), :], c_recv.at[6 + (slot - 1) * 2 + half])
        score_block(1, slot)
    for half in (0, 1):
        arrived(cen.at[1, pl.ds(3 * KS + half * 64, 64), :], c_recv.at[6 + 4 + half])
    score_block(1, 3)
    lse = exchange_lse(1)
    out_ref[...] = reduce_centers(1, lse, own)

    for copy in started:
        copy.wait_send()
    for it in range(ITERS):

        def told(k, carry):
            pltpu.make_async_remote_copy(
                src_ref=lse_all.at[it, me], dst_ref=lse_all.at[it, me],
                send_sem=l_send.at[it, k], recv_sem=l_recv.at[it, me], device_id=partner, device_id_type=MESH,
            ).wait_send()
            return carry

        lax.fori_loop(1, SRC, told, 0)


def local(vectors, block_sides, centers):
    vmem = pltpu.VMEM
    dma = pltpu.SemaphoreType.DMA
    whole = pl.BlockSpec(memory_space=pltpu.VMEM)
    return pl.pallas_call(
        kernel,
        out_shape=jax.ShapeDtypeStruct((KS, D), jnp.bfloat16),
        in_specs=[whole, pl.BlockSpec(memory_space=pltpu.SMEM), whole],
        out_specs=whole,
        scratch_shapes=[
            vmem((SRC * ROWS, D), jnp.bfloat16),
            vmem((KS, D), jnp.bfloat16),
            vmem((ITERS, 4 * KS, D), jnp.bfloat16),
            vmem((4, KS, 128), F32),
            vmem((4, SRC, KS, CHUNK), F32),
            vmem((4, SRC, CHUNK), F32),
            vmem((4, SRC, CHUNK), F32),
            vmem((4, SRC, CHUNK), F32),
            vmem((KS, 128), F32),
            vmem((ITERS, SRC, SRC, CHUNK), F32),
            vmem((ITERS, 4, KS, D), F32),
            vmem((ITERS, 2, 64, D), F32),
            vmem((ITERS, 2, KS, D), F32),
            vmem((ITERS, 4, 8, 128), F32),
            vmem((ITERS, 4, 8, 128), F32),
            dma((160,)), dma((64,)),
            dma((6 * ITERS,)), dma((6 * ITERS,)),
            dma((ITERS, SRC)), dma((ITERS, SRC)),
            dma((6 * ITERS,)), dma((6 * ITERS,)),
            dma((4 * ITERS,)), dma((4 * ITERS,)),
        ],
        compiler_params=pltpu.CompilerParams(
            collective_id=0, has_side_effects=True, vmem_limit_bytes=56 * 1024 * 1024
        ),
        name="refine",
    )(vectors, block_sides, centers)


def solution(mesh):
    in_specs = (P(("wide", "narrow"), None), P(("wide", "narrow")), P(("wide", "narrow"), None))
    out_specs = P(("wide", "narrow"), None)
    return jax.shard_map(local, mesh=mesh, in_specs=in_specs, out_specs=out_specs, check_vma=False)
```

time: 853 us -> 141 us (0.17)
  the two profiles are of different devices: /device:TPU:32 before, /device:TPU:2 now
where the time goes in v1:
time: 141 us
  Pallas kernels  140 us (99%)
  local copies, waits for them, and re-layouts  1.62 us (1%)
    pallas_call x1, Pallas kernels, local(): pl.pallas_call(kernel, out_shape=jax.ShapeDtypeStruct((KS, D), jnp.bfloat...  140 us

profile of v1, /device:TPU:2, one launch (start us, length us, event | category | flops | bytes accessed | tf_op | source)
XLA Modules:
  0.0 141.2 jit_solution(4752750069113124398)
XLA Ops:
  0.0 139.6 %refine.1 = bf16[128,768]{1,0:T(8,128)(2,1)} custom-call(bf16[256,768]{1,0:T(8,128)(2,1)} %vec_ref.1, s32[2]{0:T(128)} %sides_ref.1, bf16[128,768]{1,0:T(8,128)(2,1)} %cen_ref.1), custom_call_target="tpu_custom_call" | custom-call | tf_op jit(solution)/shard_map/refine/pallas_call | solution.py:375
  139.6 1.6 %copy.5 = bf16[128,768]{1,0:T(8,128)(2,1)} copy(bf16[128,768]{1,0:T(8,128)(2,1)} %refine.1) | data formatting | bytes 393216

commit v2 on v1

--- a/solution.py
+++ b/solution.py
@@ -18,68 +18,58 @@
 SRC = 16
 CHUNK = ROWS
 ITERS = 2
-Y_FIRST = (3,)
+UNROLL = 2
 SCALE = 4.0 / math.sqrt(D) * math.log2(math.e)
 F32 = jnp.float32
-NT = (((1,), (1,)), ((), ()))
-
-
-def hops(p, f, s):
+
+
+def sends(key):
+    p, dy, dz, dc = key
     out = []
-    if s == 0:
-        relay = 1 if p % 2 == 0 else -1
-        if f == 0:
-            out += [("f", 1), ("f", -1)]
-        elif (f == 1 and relay == 1) or (f == 3 and relay == -1):
-            out.append(("f", relay))
-        out += [("s", 1), ("s", -1)]
-    else:
-        relay = 1 if (p + f) % 2 == 0 else -1
-        if (s == 1 and relay == 1) or (s == 3 and relay == -1):
-            out.append(("s", relay))
+    if dc == 1:
+        return out
+    if dy == 0 and dz == 0:
+        out.append(("z+" if p % 2 == 0 else "z-", ("relay", p)))
+    relay = 1 if (p + dz) % 2 == 0 else -1
+    if dy == 0:
+        out += [("y+", (p, 1, dz, 0)), ("y-", (p, 3, dz, 0))]
+    elif (dy == 1 and relay == 1) or (dy == 3 and relay == -1):
+        out.append(("y+" if relay == 1 else "y-", (p, 2, dz, 0)))
+    out.append(("c", (p, dy, dz, 1)))
     return out
 
 
-def sends(key):
-    p, dy, dz = key
-    y_first = p in Y_FIRST
-    f, s = (dy, dz) if y_first else (dz, dy)
-    res = []
-    for dim, step in hops(p, f, s):
-        nf, ns = ((f + step) % 4, s) if dim == "f" else (f, (s + step) % 4)
-        axis = ("y" if dim == "f" else "z") if y_first else ("z" if dim == "f" else "y")
-        res.append((axis, step, (p, nf, ns) if y_first else (p, ns, nf)))
-    return res
-
-
 def plan():
-    cost = {"y": 2.1, "z": 4.2}
-    lat = {"y": 1.7, "z": 2.4}
+    cost = {"y+": 2.1, "y-": 2.1, "z+": 4.2, "z-": 4.2, "c": 0.4}
+    lat = {"y+": 1.7, "y-": 1.7, "z+": 2.4, "z-": 2.4, "c": 1.0}
     free = {}
-    heap = [(0.0, 0, (0, 0, 0)), (0.0, 1, (1, 0, 0)), (5.0, 2, (2, 0, 0)), (7.0, 3, (3, 0, 0))]
+    heap = [(0.0, 0, (0, 0, 0, 0)), (0.0, 1, (1, 0, 0, 0)), (6.0, 2, (2, 0, 0, 0)), (8.0, 3, (3, 0, 0, 0))]
     count = 4
     order = []
     while heap:
         now, unused, key = heapq.heappop(heap)
         order.append(key)
-        for axis, step, target in sends(key):
-            link = (axis, step)
+        if key[0] == "relay":
+            out = [("z+" if key[1] % 2 == 0 else "z-", (key[1], 0, 1, 0))]
+        else:
+            out = sends(key)
+        for link, target in out:
             start = max(now, free.get(link, 0.0))
-            free[link] = start + cost[axis]
-            heapq.heappush(heap, (free[link] + lat[axis], count, target))
+            free[link] = start + cost[link]
+            heapq.heappush(heap, (free[link] + lat[link], count, target))
             count += 1
     return order, max(free.values())
 
 
 def sem_of(key):
-    p, dy, dz = key
-    return p * 16 + dy * 4 + dz
+    p, dy, dz, dc = key
+    return p * 16 + dy * 4 + dz * 2 + dc
 
 
 def kernel(
     vec_ref, sides_ref, cen_ref, out_ref,
-    x_all, swap_out, cen, hn, e_all, m_all, l_all, f_one, den_acc, lse_all, num, relay_in, main_in, den_out, den_in,
-    x_send, x_recv, c_send, c_recv, l_send, l_recv, n_send, n_recv, d_send, d_recv,
+    x_all, xt_all, swap_out, keep_out, relay_x, fin, cen, hn, e_all, m_all, l_all, f_one, den_acc, lse_all, num, relay_in, main_in, den_out, den_in,
+    x_send, x_recv, r_send, r_recv, f_send, f_recv, c_send, c_recv, l_send, l_recv, n_send, n_recv, d_send, d_recv,
 ):
     wide = lax.axis_index("wide")
     narrow = lax.axis_index("narrow")
@@ -87,31 +77,46 @@
     z = lax.rem(wide // 2, 8)
     y = lax.rem(narrow // 4, 2) * 2 + wide // 16
     x = lax.rem(narrow, 4)
-    zp = z // 2
+    zq = z // 4
+    rest = lax.rem(z, 4)
     parity = lax.rem(z, 2)
-    me = y * 4 + zp
-
-    def device(dx, ny, nz):
+    native = core == rest // 2
+    foreign = core != rest // 2
+    away = jnp.where(native, 0, 1)
+    me = y * 4 + zq * 2 + core
+
+    def device(dx, ny, nz, ncore):
         nx = lax.rem(x + dx + 4, 4)
-        return (lax.rem(ny, 2) * 16 + nz * 2 + core, (ny // 2) * 4 + nx)
-
-    def plane(dy, dz):
-        return device(0, lax.rem(y + dy + 4, 4), lax.rem(z + 2 * dz + 8, 8))
+        return (lax.rem(ny, 2) * 16 + nz * 2 + ncore, (ny // 2) * 4 + nx)
+
+    def up(dy, dz, ncore):
+        return device(0, lax.rem(y + dy + 4, 4), lax.rem(z + dz + 8, 8), ncore)
 
     def peer(index):
-        return device(0, index // 4, lax.rem(index, 4) * 2 + parity)
+        return device(0, index // 4, lax.rem(index // 2, 2) * 4 + rest, lax.rem(index, 2))
 
     def across(dx):
-        return device(dx, y, z)
-
-    partner = device(0, y, z + 1 - 2 * parity)
+        return device(dx, y, z, core)
+
+    z_near = z + 1 - 2 * parity
+    z_outer = lax.rem(z - 1 + 2 * parity + 8, 8)
+    z_second = z + 2 - 4 * (rest // 2)
+    near = device(0, y, z_near, 1 - core)
+    outer = device(0, y, z_outer, 1 - core)
+    second = device(0, y, z_second, core)
+    mirror = device(0, y, z_second, 1 - core)
 
     first = vec_ref[0:KS, :]
-    second = vec_ref[KS : 2 * KS, :]
+    other_half = vec_ref[KS : 2 * KS, :]
     first_stays = sides_ref[0] == parity
+    keep_out[...] = jnp.where(first_stays, first, other_half)
+    swap_out[...] = jnp.where(first_stays, other_half, first)
     base = pl.multiple_of(me * ROWS, ROWS)
-    x_all[pl.ds(base, KS), :] = jnp.where(first_stays, first, second)
-    swap_out[...] = jnp.where(first_stays, second, first)
+
+    @pl.when(native)
+    def _():
+        x_all[pl.ds(base, KS), :] = keep_out[...]
+        cen[0, 0:KS, :] = cen_ref[...]
 
     barrier = pltpu.get_barrier_semaphore()
 
@@ -120,9 +125,9 @@
         return carry
 
     lax.fori_loop(1, SRC, greet, 0)
-    for other in (partner, across(1), across(-1), across(2)):
+    for other in (near, outer, mirror, up(0, 2, core), up(0, -2, core), across(1), across(-1), across(2)):
         pl.semaphore_signal(barrier, inc=1, device_id=other, device_id_type=MESH)
-    pl.semaphore_wait(barrier, SRC + 3)
+    pl.semaphore_wait(barrier, SRC - 1 + 8)
 
     started = []
 
@@ -135,20 +140,41 @@
 
     def arrived(dst, sem):
         pltpu.make_async_remote_copy(
-            src_ref=dst, dst_ref=dst, send_sem=sem, recv_sem=sem, device_id=partner, device_id_type=MESH
+            src_ref=dst, dst_ref=dst, send_sem=sem, recv_sem=sem, device_id=near, device_id_type=MESH
         ).wait_recv()
 
     def piece(source, p):
         return x_all.at[pl.ds(pl.multiple_of(source * ROWS + p * PIECE, PIECE), PIECE), :]
 
-    def source_of(dy, dz):
-        return lax.rem(y - dy + 4, 4) * 4 + lax.rem(zp - dz + 4, 4)
-
+    def source_of(dy, dz, dc):
+        nz = zq if dz == 0 else 1 - zq
+        return lax.rem(y - dy + 4, 4) * 4 + nz * 2 + (core if dc == 0 else 1 - core)
+
+    to = tuple(jnp.where(native, a, b) for a, b in zip(near, outer))
+    target = y * 4 + jnp.where(native, zq, z_outer // 4) * 2 + 1 - core
     for half in (0, 1):
         send(
-            swap_out.at[pl.ds(half * PIECE, PIECE), :], piece(me, 2 + half),
-            x_send.at[sem_of((2 + half, 0, 0))], x_recv.at[sem_of((2 + half, 0, 0))], partner,
+            swap_out.at[pl.ds(half * PIECE, PIECE), :],
+            x_all.at[pl.ds(pl.multiple_of(target * ROWS + away * KS + half * PIECE, PIECE), PIECE), :],
+            x_send.at[half], x_recv.at[(2 * away + half) * 16], to,
         )
+
+    def foreign_copies():
+        yield pltpu.make_async_remote_copy(
+            src_ref=cen_ref, dst_ref=cen.at[0, pl.ds(0, KS), :], send_sem=f_send.at[2], recv_sem=f_recv.at[0],
+            device_id=mirror, device_id_type=MESH,
+        )
+        for half in (0, 1):
+            yield pltpu.make_async_remote_copy(
+                src_ref=keep_out.at[pl.ds(half * PIECE, PIECE), :], dst_ref=piece(me, 2 + half),
+                send_sem=f_send.at[half], recv_sem=x_recv.at[(2 + half) * 16],
+                device_id=second, device_id_type=MESH,
+            )
+
+    @pl.when(foreign)
+    def _():
+        for copy in foreign_copies():
+            copy.start()
 
     def send_centers(it, own):
         for step, slot in ((1, 1), (-1, 2)):
@@ -184,27 +210,26 @@
         m_all[q, pl.ds(r, 1), :] = top
         l_all[q, pl.ds(r, 1), :] = jnp.sum(e, axis=0, keepdims=True)
 
-    def scores(it, q, r):
-        rows = x_all[pl.ds(pl.multiple_of(r * CHUNK, CHUNK), CHUNK), :]
-        product = lax.dot_general(
-            cen[it, pl.ds(q * KS, KS), :], rows, NT, preferred_element_type=F32
-        )
-        exponents(q, r, product)
-
     def score_chunk(r):
-        rows = x_all[pl.ds(pl.multiple_of(r * CHUNK, CHUNK), CHUNK), :]
+        xt_all[r] = x_all[pl.ds(pl.multiple_of(r * CHUNK, CHUNK), CHUNK), :].T
         for q in range(4):
-            product = lax.dot_general(cen[0, pl.ds(q * KS, KS), :], rows, NT, preferred_element_type=F32)
-            exponents(q, r, product)
-
-    def score_block(it, q):
-        norms(it, q)
-
-        def one(r, carry):
-            scores(it, q, r)
+            exponents(q, r, jnp.dot(cen[0, pl.ds(q * KS, KS), :], xt_all[r], preferred_element_type=F32))
+
+    def score_block(it, q, count=1):
+        for k in range(count):
+            norms(it, q + k)
+
+        def one(g, carry):
+            for j in range(UNROLL):
+                r = g * UNROLL + j
+                product = jnp.dot(
+                    cen[it, pl.ds(q * KS, count * KS), :], xt_all[r], preferred_element_type=F32
+                )
+                for k in range(count):
+                    exponents(q + k, r, product[k * KS : (k + 1) * KS, :])
             return carry
 
-        lax.fori_loop(0, SRC, one, 0)
+        lax.fori_loop(0, SRC // UNROLL, one, 0)
 
     def exchange_lse(it):
         top = jnp.maximum(jnp.maximum(m_all[0], m_all[1]), jnp.maximum(m_all[2], m_all[3]))
@@ -305,27 +330,49 @@
         return ((total + old[...].astype(F32)) / (column + 1.0)).astype(jnp.bfloat16)
 
     order, unused = plan()
+    mine = cen.at[0, pl.ds(0, KS), :]
     seen = {}
-    send_centers(0, cen_ref)
-    cen[0, 0:KS, :] = cen_ref[...]
-    norms(0, 0)
     ready = []
     centers_in = False
     for number, key in enumerate(order):
-        p, dy, dz = key
-        source = source_of(dy, dz)
-        if key not in ((0, 0, 0), (1, 0, 0)):
+        if key[0] == "relay":
+            p = key[1]
+            step = 2 if p % 2 == 0 else -2
+            arrived(relay_x.at[p], r_recv.at[p])
+            origin = y * 4 + lax.rem(z - step + 8, 8) // 4 * 2 + core
+            send(relay_x.at[p], piece(origin, p), r_send.at[4 + p], x_recv.at[sem_of((p, 0, 1, 0))], up(0, step, core))
+            continue
+        p, dy, dz, dc = key
+        source = source_of(dy, dz, dc)
+        if key in ((0, 0, 0, 0), (1, 0, 0, 0)):
+
+            @pl.when(foreign)
+            def _():
+                arrived(piece(source, p), x_recv.at[sem_of(key)])
+
+        else:
             arrived(piece(source, p), x_recv.at[sem_of(key)])
-        for axis, step, target in sends(key):
-            to = plane(step, 0) if axis == "y" else plane(0, step)
-            index = len([c for c in started if c is not None])
-            send(piece(source, p), piece(source, p), x_send.at[64 + index - 6], x_recv.at[sem_of(target)], to)
-        seen[(dy, dz)] = seen.get((dy, dz), 0) + 1
-        if seen[(dy, dz)] == PIECES:
+        for link, goal in sends(key):
+            if goal[0] == "relay":
+                step = 2 if p % 2 == 0 else -2
+                send(piece(source, p), relay_x.at[p], r_send.at[p], r_recv.at[p], up(0, step, core))
+            else:
+                to = up(0, 0, 1 - core) if link == "c" else up(1 if link == "y+" else -1, 0, core)
+                send(piece(source, p), piece(source, p), x_send.at[len(started)], x_recv.at[sem_of(goal)], to)
+        seen[(dy, dz, dc)] = seen.get((dy, dz, dc), 0) + 1
+        if seen[(dy, dz, dc)] == PIECES:
             ready.append(source)
-        if number == 3:
+        if key == (1, 0, 0, 0):
+
+            @pl.when(foreign)
+            def _():
+                arrived(mine, f_recv.at[0])
+
+            send_centers(0, mine)
+            norms(0, 0)
+        if number == 8:
             relay_centers(0)
-        if number >= 12 and not centers_in:
+        if number >= 16 and not centers_in:
             for index in (1, 2, 4, 5):
                 slot, half = ((index // 2) + 1, index % 2) if index < 4 else (3, index - 4)
                 arrived(cen.at[0, pl.ds(slot * KS + half * 64, 64), :], c_recv.at[index])
@@ -337,7 +384,7 @@
                 score_chunk(r)
             ready = []
     lse = exchange_lse(0)
-    fresh = reduce_centers(0, lse, cen_ref)
+    fresh = reduce_centers(0, lse, mine)
 
     cen[1, 0:KS, :] = fresh
     own = cen.at[1, pl.ds(0, KS), :]
@@ -347,12 +394,27 @@
     for slot in (1, 2):
         half = 2 - slot
         arrived(cen.at[1, pl.ds(slot * KS + half * 64, 64), :], c_recv.at[6 + (slot - 1) * 2 + half])
-        score_block(1, slot)
+    score_block(1, 1, 2)
     for half in (0, 1):
         arrived(cen.at[1, pl.ds(3 * KS + half * 64, 64), :], c_recv.at[6 + 4 + half])
     score_block(1, 3)
     lse = exchange_lse(1)
-    out_ref[...] = reduce_centers(1, lse, own)
+    fin[...] = reduce_centers(1, lse, own)
+
+    @pl.when(native)
+    def _():
+        out_ref[...] = fin[...]
+
+    @pl.when(foreign)
+    def _():
+        home = pltpu.make_async_remote_copy(
+            src_ref=fin, dst_ref=out_ref, send_sem=f_send.at[3], recv_sem=f_recv.at[1],
+            device_id=mirror, device_id_type=MESH,
+        )
+        home.start()
+        home.wait()
+        for copy in foreign_copies():
+            copy.wait_send()
 
     for copy in started:
         copy.wait_send()
@@ -361,7 +423,7 @@
         def told(k, carry):
             pltpu.make_async_remote_copy(
                 src_ref=lse_all.at[it, me], dst_ref=lse_all.at[it, me],
-                send_sem=l_send.at[it, k], recv_sem=l_recv.at[it, me], device_id=partner, device_id_type=MESH,
+                send_sem=l_send.at[it, k], recv_sem=l_recv.at[it, me], device_id=near, device_id_type=MESH,
             ).wait_send()
             return carry
 
@@ -379,6 +441,10 @@
         out_specs=whole,
         scratch_shapes=[
             vmem((SRC * ROWS, D), jnp.bfloat16),
+            vmem((SRC, D, CHUNK), jnp.bfloat16),
+            vmem((KS, D), jnp.bfloat16),
+            vmem((KS, D), jnp.bfloat16),
+            vmem((PIECES, PIECE, D), jnp.bfloat16),
             vmem((KS, D), jnp.bfloat16),
             vmem((ITERS, 4 * KS, D), jnp.bfloat16),
             vmem((4, KS, 128), F32),
@@ -394,6 +460,8 @@
             vmem((ITERS, 4, 8, 128), F32),
             vmem((ITERS, 4, 8, 128), F32),
             dma((160,)), dma((64,)),
+            dma((8,)), dma((4,)),
+            dma((4,)), dma((2,)),
             dma((6 * ITERS,)), dma((6 * ITERS,)),
             dma((ITERS, SRC)), dma((ITERS, SRC)),
             dma((6 * ITERS,)), dma((6 * ITERS,)),

time: 141 us -> 136 us (0.965)
  the two profiles are of different devices: /device:TPU:2 before, /device:TPU:1 now
where the time goes in v2:
time: 136 us; the launch traced here: 135 us
  Pallas kernels  134 us (99%)
  local copies, waits for them, and re-layouts  1.62 us (1%)
    pallas_call x1, Pallas kernels, local(): pl.pallas_call(kernel, out_shape=jax.ShapeDtypeStruct((KS, D), jnp.bfloat...  134 us

profile of v2, /device:TPU:1, one launch (start us, length us, event | category | flops | bytes accessed | tf_op | source)
XLA Modules:
  0.0 135.2 jit_solution(18034567332713117590)
XLA Ops:
  0.0 133.6 %refine.1 = bf16[128,768]{1,0:T(8,128)(2,1)} custom-call(bf16[256,768]{1,0:T(8,128)(2,1)} %vec_ref.1, s32[2]{0:T(128)} %sides_ref.1, bf16[128,768]{1,0:T(8,128)(2,1)} %cen_ref.1), custom_call_target="tpu_custom_call" | custom-call | tf_op jit(solution)/shard_map/refine/pallas_call | solution.py:437
  133.6 1.6 %copy.5 = bf16[128,768]{1,0:T(8,128)(2,1)} copy(bf16[128,768]{1,0:T(8,128)(2,1)} %refine.1) | data formatting | bytes 393216

commit v3 on v2

--- a/solution.py
+++ b/solution.py
@@ -19,6 +19,9 @@
 CHUNK = ROWS
 ITERS = 2
 UNROLL = 2
+LOW = (True, False)
+AT = (22, 30, 38)
+BF16 = jnp.bfloat16
 SCALE = 4.0 / math.sqrt(D) * math.log2(math.e)
 F32 = jnp.float32
 
@@ -68,8 +71,9 @@
 
 def kernel(
     vec_ref, sides_ref, cen_ref, out_ref,
-    x_all, xt_all, swap_out, keep_out, relay_x, fin, cen, hn, e_all, m_all, l_all, f_one, den_acc, lse_all, num, relay_in, main_in, den_out, den_in,
-    x_send, x_recv, r_send, r_recv, f_send, f_recv, c_send, c_recv, l_send, l_recv, n_send, n_recv, d_send, d_recv,
+    x_all, xt_all, swap_out, keep_out, relay_x, fin, cen, hn, e_all, m_all, l_all, f_one, den_acc, lse_two, lse_all, num, num_low,
+    relay_f32, main_f32, relay_low, main_low, den_out, den_in,
+    x_send, x_recv, go_sem, r_send, r_recv, f_send, f_recv, c_send, c_recv, l_send, l_recv, n_send, n_recv, d_send, d_recv,
 ):
     wide = lax.axis_index("wide")
     narrow = lax.axis_index("narrow")
@@ -120,14 +124,14 @@
 
     barrier = pltpu.get_barrier_semaphore()
 
-    def greet(k, carry):
-        pl.semaphore_signal(barrier, inc=1, device_id=peer(lax.rem(me + k, SRC)), device_id_type=MESH)
-        return carry
-
-    lax.fori_loop(1, SRC, greet, 0)
-    for other in (near, outer, mirror, up(0, 2, core), up(0, -2, core), across(1), across(-1), across(2)):
+    around = [up(dy, 0, core) for dy in (1, -1)] + [across(1), across(-1), up(0, 0, 1 - core)]
+    around += [up(0, dz, c) for dz in (1, -1) for c in (core, 1 - core)]
+    for other in around:
         pl.semaphore_signal(barrier, inc=1, device_id=other, device_id_type=MESH)
-    pl.semaphore_wait(barrier, SRC - 1 + 8)
+    pl.semaphore_wait(barrier, len(around))
+    for dz in (1, -1):
+        pl.semaphore_signal(go_sem, inc=1, device_id=up(0, dz, core), device_id_type=MESH)
+    pl.semaphore_wait(go_sem, 2)
 
     started = []
 
@@ -159,22 +163,22 @@
             x_send.at[half], x_recv.at[(2 * away + half) * 16], to,
         )
 
-    def foreign_copies():
-        yield pltpu.make_async_remote_copy(
+    def foreign_rows(half):
+        return pltpu.make_async_remote_copy(
+            src_ref=keep_out.at[pl.ds(half * PIECE, PIECE), :], dst_ref=piece(me, 2 + half),
+            send_sem=f_send.at[half], recv_sem=x_recv.at[(2 + half) * 16], device_id=second, device_id_type=MESH,
+        )
+
+    def foreign_centers():
+        return pltpu.make_async_remote_copy(
             src_ref=cen_ref, dst_ref=cen.at[0, pl.ds(0, KS), :], send_sem=f_send.at[2], recv_sem=f_recv.at[0],
             device_id=mirror, device_id_type=MESH,
         )
-        for half in (0, 1):
-            yield pltpu.make_async_remote_copy(
-                src_ref=keep_out.at[pl.ds(half * PIECE, PIECE), :], dst_ref=piece(me, 2 + half),
-                send_sem=f_send.at[half], recv_sem=x_recv.at[(2 + half) * 16],
-                device_id=second, device_id_type=MESH,
-            )
 
     @pl.when(foreign)
     def _():
-        for copy in foreign_copies():
-            copy.start()
+        foreign_rows(0).start()
+        foreign_rows(1).start()
 
     def send_centers(it, own):
         for step, slot in ((1, 1), (-1, 2)):
@@ -231,87 +235,104 @@
 
         lax.fori_loop(0, SRC // UNROLL, one, 0)
 
+    def log_add(parts):
+        best = functools.reduce(jnp.maximum, parts)
+        return best + jnp.log2(sum(jnp.exp2(part - best) for part in parts))
+
+    def lse_copy(it, k):
+        other = lax.rem(me // 2 + k, SRC // 2)
+        return pltpu.make_async_remote_copy(
+            src_ref=lse_all.at[it, me // 2], dst_ref=lse_all.at[it, me // 2],
+            send_sem=l_send.at[it, k], recv_sem=l_recv.at[it, me // 2],
+            device_id=peer(other * 2 + core), device_id_type=MESH,
+        )
+
     def exchange_lse(it):
         top = jnp.maximum(jnp.maximum(m_all[0], m_all[1]), jnp.maximum(m_all[2], m_all[3]))
         total = sum(l_all[q] * jnp.exp2(m_all[q] - top) for q in range(4))
-        lse_all[it, me] = top + jnp.log2(total)
+        lse_two[it, 0] = top + jnp.log2(total)
+        send(lse_two.at[it, 0], lse_two.at[it, 1], l_send.at[it, 0], l_recv.at[it, SRC // 2], up(0, 0, 1 - core))
+        arrived(lse_two.at[it, 1], l_recv.at[it, SRC // 2])
+        lse_all[it, me // 2] = log_add([lse_two[it, 0], lse_two[it, 1]])
 
         def tell(k, carry):
-            pltpu.make_async_remote_copy(
-                src_ref=lse_all.at[it, me], dst_ref=lse_all.at[it, me],
-                send_sem=l_send.at[it, k], recv_sem=l_recv.at[it, me],
-                device_id=peer(lax.rem(me + k, SRC)), device_id_type=MESH,
-            ).start()
+            lse_copy(it, k).start()
             return carry
 
-        lax.fori_loop(1, SRC, tell, 0)
+        lax.fori_loop(1, SRC // 2, tell, 0)
 
         def hear(k, carry):
-            other = lax.rem(me + k, SRC)
+            other = lax.rem(me // 2 + k, SRC // 2)
             arrived(lse_all.at[it, other], l_recv.at[it, other])
             return carry
 
-        lax.fori_loop(1, SRC, hear, 0)
-        best = lse_all[it, 0]
-        for k in range(1, SRC):
-            best = jnp.maximum(best, lse_all[it, k])
-        total = jnp.exp2(lse_all[it, 0] - best)
-        for k in range(1, SRC):
-            total = total + jnp.exp2(lse_all[it, k] - best)
-        return best + jnp.log2(total)
-
-    def weigh(it, q, lse):
-        f_one[q] = jnp.exp2(m_all[q] - lse)
-
-        def group(g):
-            parts = []
-            den = jnp.zeros((KS, 128), F32)
-            for j in range(4):
-                r = g * 4 + j
-                weights = (e_all[q, r] * f_one[q, pl.ds(r, 1), :]).astype(jnp.bfloat16)
-                wide_weights = weights.astype(F32)
-                den = den + wide_weights[:, :128] + wide_weights[:, 128:]
-                parts.append(weights)
+        lax.fori_loop(1, SRC // 2, hear, 0)
+        return log_add([lse_all[it, k] for k in range(SRC // 2)])
+
+    def weigh(it, q, lse, count=1):
+        blocks = range(count)
+        for k in blocks:
+            f_one[q + k] = jnp.exp2(m_all[q + k] - lse)
+
+        def group(g, first):
+            lines = []
+            for k in blocks:
+                parts = []
+                den = jnp.zeros((KS, 128), F32)
+                for j in range(4):
+                    r = g * 4 + j
+                    weights = (e_all[q + k, r] * f_one[q + k, pl.ds(r, 1), :]).astype(BF16)
+                    wide_weights = weights.astype(F32)
+                    den = den + wide_weights[:, :128] + wide_weights[:, 128:]
+                    parts.append(weights)
+                lines.append(jnp.concatenate(parts, axis=1))
+                den_acc[q + k] = den if first else den_acc[q + k] + den
             rows = x_all[pl.ds(pl.multiple_of(g * 4 * CHUNK, 4 * CHUNK), 4 * CHUNK), :]
-            term = jnp.dot(jnp.concatenate(parts, axis=1), rows, preferred_element_type=F32)
-            return term, den
-
-        num[it, q], den_acc[...] = group(0)
+            weights = lines[0] if count == 1 else jnp.concatenate(lines, axis=0)
+            term = jnp.dot(weights, rows, preferred_element_type=F32)
+            for k in blocks:
+                part = term[k * KS : (k + 1) * KS, :]
+                num[it, q + k] = part if first else num[it, q + k] + part
+
+        group(0, True)
 
         def one(g, carry):
-            term, den = group(g)
-            num[it, q] += term
-            den_acc[...] += den
+            group(g, False)
             return carry
 
         lax.fori_loop(1, 4, one, 0)
-        column = jnp.sum(den_acc[...], axis=1, keepdims=True)
         here = lax.broadcasted_iota(jnp.int32, (KS, 128), 0) == lax.broadcasted_iota(jnp.int32, (KS, 128), 1)
-        row = jnp.sum(jnp.where(here, column, 0.0), axis=0, keepdims=True)
-        den_out[it, q] = jnp.broadcast_to(row, (8, 128))
+        for k in blocks:
+            column = jnp.sum(den_acc[q + k], axis=1, keepdims=True)
+            row = jnp.sum(jnp.where(here, column, 0.0), axis=0, keepdims=True)
+            den_out[it, q + k] = jnp.broadcast_to(row, (8, 128))
+            if LOW[it] and q + k > 0:
+                num_low[it, q + k] = num[it, q + k].astype(BF16)
 
     def reduce_centers(it, lse, old):
+        table, relay_in, main_in = (num_low, relay_low, main_low) if LOW[it] else (num, relay_f32, main_f32)
         weigh(it, 3, lse)
         base = it * 6
         for i, (half, step) in enumerate(((0, 1), (1, -1))):
             send(
-                num.at[it, 3, pl.ds(half * 64, 64), :], relay_in.at[it, i],
+                table.at[it, 3, pl.ds(half * 64, 64), :], relay_in.at[it, i],
                 n_send.at[base + i], n_recv.at[base + i], across(step),
             )
         send(den_out.at[it, 3], den_in.at[it, 3], d_send.at[it * 4 + 3], d_recv.at[it * 4 + 3], across(2))
+        weigh(it, 1, lse, 2)
         for i, (q, step, half) in enumerate(((2, 1, 1), (1, -1, 0))):
-            weigh(it, q, lse)
             send(
-                num.at[it, q, pl.ds(half * 64, 64), :], main_in.at[it, i, pl.ds(half * 64, 64), :],
+                table.at[it, q, pl.ds(half * 64, 64), :], main_in.at[it, i, pl.ds(half * 64, 64), :],
                 n_send.at[base + 2 + i], n_recv.at[base + 2 + i], across(step),
             )
             send(den_out.at[it, q], den_in.at[it, 3 - q], d_send.at[it * 4 + q], d_recv.at[it * 4 + 3 - q], across(step))
         for i, (q, step, half) in enumerate(((2, 1, 0), (1, -1, 1))):
             rows = pl.ds(half * 64, 64)
             arrived(relay_in.at[it, i], n_recv.at[base + i])
-            num[it, q, rows, :] += relay_in[it, i]
+            part = num[it, q, rows, :] + relay_in[it, i].astype(F32)
+            table[it, q, rows, :] = part.astype(table.dtype)
             send(
-                num.at[it, q, rows, :], main_in.at[it, i, rows, :],
+                table.at[it, q, rows, :], main_in.at[it, i, rows, :],
                 n_send.at[base + 4 + i], n_recv.at[base + 4 + i], across(step),
             )
         weigh(it, 0, lse)
@@ -326,14 +347,14 @@
         for i, half in enumerate((0, 1)):
             rows = pl.ds(half * 64, 64)
             arrived(main_in.at[it, i, rows, :], n_recv.at[base + 4 + i])
-        total = num[it, 0] + main_in[it, 0] + main_in[it, 1]
-        return ((total + old[...].astype(F32)) / (column + 1.0)).astype(jnp.bfloat16)
+        total = num[it, 0] + main_in[it, 0].astype(F32) + main_in[it, 1].astype(F32)
+        return ((total + old[...].astype(F32)) / (column + 1.0)).astype(BF16)
 
     order, unused = plan()
     mine = cen.at[0, pl.ds(0, KS), :]
     seen = {}
     ready = []
-    centers_in = False
+    phase = 0
     for number, key in enumerate(order):
         if key[0] == "relay":
             p = key[1]
@@ -362,7 +383,13 @@
         seen[(dy, dz, dc)] = seen.get((dy, dz, dc), 0) + 1
         if seen[(dy, dz, dc)] == PIECES:
             ready.append(source)
-        if key == (1, 0, 0, 0):
+        if key == (3, 0, 0, 0):
+
+            @pl.when(foreign)
+            def _():
+                foreign_centers().start()
+
+        if number >= AT[0] and phase == 0:
 
             @pl.when(foreign)
             def _():
@@ -370,19 +397,22 @@
 
             send_centers(0, mine)
             norms(0, 0)
-        if number == 8:
+            phase = 1
+        if number >= AT[1] and phase == 1:
             relay_centers(0)
-        if number >= 16 and not centers_in:
+            phase = 2
+        if number >= AT[2] and phase == 2:
             for index in (1, 2, 4, 5):
                 slot, half = ((index // 2) + 1, index % 2) if index < 4 else (3, index - 4)
                 arrived(cen.at[0, pl.ds(slot * KS + half * 64, 64), :], c_recv.at[index])
             for q in (1, 2, 3):
                 norms(0, q)
-            centers_in = True
-        if centers_in:
-            for r in ready:
-                score_chunk(r)
-            ready = []
+            phase = 3
+        if phase == 3:
+            if ready:
+                score_chunk(ready.pop(0))
+    for r in ready:
+        score_chunk(r)
     lse = exchange_lse(0)
     fresh = reduce_centers(0, lse, mine)
 
@@ -413,7 +443,7 @@
         )
         home.start()
         home.wait()
-        for copy in foreign_copies():
+        for copy in (foreign_rows(0), foreign_rows(1), foreign_centers()):
             copy.wait_send()
 
     for copy in started:
@@ -421,13 +451,10 @@
     for it in range(ITERS):
 
         def told(k, carry):
-            pltpu.make_async_remote_copy(
-                src_ref=lse_all.at[it, me], dst_ref=lse_all.at[it, me],
-                send_sem=l_send.at[it, k], recv_sem=l_recv.at[it, me], device_id=near, device_id_type=MESH,
-            ).wait_send()
+            lse_copy(it, k).wait_send()
             return carry
 
-        lax.fori_loop(1, SRC, told, 0)
+        lax.fori_loop(1, SRC // 2, told, 0)
 
 
 def local(vectors, block_sides, centers):
@@ -452,14 +479,19 @@
             vmem((4, SRC, CHUNK), F32),
             vmem((4, SRC, CHUNK), F32),
             vmem((4, SRC, CHUNK), F32),
-            vmem((KS, 128), F32),
-            vmem((ITERS, SRC, SRC, CHUNK), F32),
+            vmem((4, KS, 128), F32),
+            vmem((ITERS, 2, SRC, CHUNK), F32),
+            vmem((ITERS, SRC // 2, SRC, CHUNK), F32),
             vmem((ITERS, 4, KS, D), F32),
+            vmem((ITERS, 4, KS, D), BF16),
             vmem((ITERS, 2, 64, D), F32),
             vmem((ITERS, 2, KS, D), F32),
+            vmem((ITERS, 2, 64, D), BF16),
+            vmem((ITERS, 2, KS, D), BF16),
             vmem((ITERS, 4, 8, 128), F32),
             vmem((ITERS, 4, 8, 128), F32),
             dma((160,)), dma((64,)),
+            pltpu.SemaphoreType.REGULAR,
             dma((8,)), dma((4,)),
             dma((4,)), dma((2,)),
             dma((6 * ITERS,)), dma((6 * ITERS,)),

time: 136 us -> 128 us (0.941)
  Pallas kernels: 134 us -> 124 us
    pallas_call x1, Pallas kernels: 134 us -> 124 us  [local(): pl.pallas_call(kernel, out_shape=jax.ShapeDtypeStruct((KS, D), jnp.bfloat...]
where the time goes in v3:
time: 128 us; the launch traced here: 126 us
  Pallas kernels  124 us (97%)
  local copies, waits for them, and re-layouts  1.62 us (1%)
    pallas_call x1, Pallas kernels, local(): pl.pallas_call(kernel, out_shape=jax.ShapeDtypeStruct((KS, D), jnp.bfloat...  124 us

profile of v3, /device:TPU:1, one launch (start us, length us, event | category | flops | bytes accessed | tf_op | source)
XLA Modules:
  0.0 126.0 jit_solution(7012233820938651080)
XLA Ops:
  0.0 124.4 %refine.1 = bf16[128,768]{1,0:T(8,128)(2,1)} custom-call(bf16[256,768]{1,0:T(8,128)(2,1)} %vec_ref.1, s32[2]{0:T(128)} %sides_ref.1, bf16[128,768]{1,0:T(8,128)(2,1)} %cen_ref.1), custom_call_target="tpu_custom_call" | custom-call | tf_op jit(solution)/shard_map/refine/pallas_call | solution.py:464
  124.4 1.6 %copy.5 = bf16[128,768]{1,0:T(8,128)(2,1)} copy(bf16[128,768]{1,0:T(8,128)(2,1)} %refine.1) | data formatting | bytes 393216

commit v4 on v3

--- a/solution.py
+++ b/solution.py
@@ -20,7 +20,11 @@
 ITERS = 2
 UNROLL = 2
 LOW = (True, False)
-AT = (22, 30, 38)
+MIRROR = 17.0
+MIRROR_AFTER = (1, 0, 0, 0)
+COST = (2.1, 3.6, 0.4)
+LATC = 4.0
+START = (2.0, 4.0, 6.5, 8.5)
 BF16 = jnp.bfloat16
 SCALE = 4.0 / math.sqrt(D) * math.log2(math.e)
 F32 = jnp.float32
@@ -43,17 +47,22 @@
 
 
 def plan():
-    cost = {"y+": 2.1, "y-": 2.1, "z+": 4.2, "z-": 4.2, "c": 0.4}
-    lat = {"y+": 1.7, "y-": 1.7, "z+": 2.4, "z-": 2.4, "c": 1.0}
+    cost = {"y+": COST[0], "y-": COST[0], "z+": COST[1], "z-": COST[1], "c": COST[2], "x+": 2.1, "x-": 2.1}
+    lat = {"y+": 1.7, "y-": 1.7, "z+": 2.4, "z-": 2.4, "c": LATC, "x+": 1.7, "x-": 1.7}
     free = {}
-    heap = [(0.0, 0, (0, 0, 0, 0)), (0.0, 1, (1, 0, 0, 0)), (6.0, 2, (2, 0, 0, 0)), (8.0, 3, (3, 0, 0, 0))]
-    count = 4
+    heap = [(when, p, (p, 0, 0, 0)) for p, when in enumerate(START)]
+    heap.append((MIRROR, 4, ("mirror",)))
+    count = 5
     order = []
     while heap:
         now, unused, key = heapq.heappop(heap)
         order.append(key)
         if key[0] == "relay":
             out = [("z+" if key[1] % 2 == 0 else "z-", (key[1], 0, 1, 0))]
+        elif key[0] == "mirror":
+            out = [("x+", ("cen", 1, 0)), ("x-", ("cen", 2, 1)), ("x+", ("cen", 1, 1)), ("x-", ("cen", 2, 0))]
+        elif key[0] == "cen":
+            out = [("x+" if key[1] == 1 else "x-", ("cen", 3, key[2]))] if key[1:] in ((1, 0), (2, 1)) else []
         else:
             out = sends(key)
         for link, target in out:
@@ -115,7 +124,7 @@
     first_stays = sides_ref[0] == parity
     keep_out[...] = jnp.where(first_stays, first, other_half)
     swap_out[...] = jnp.where(first_stays, other_half, first)
-    base = pl.multiple_of(me * ROWS, ROWS)
+    base = pl.multiple_of(me // 2 * (2 * ROWS) + core * KS, KS)
 
     @pl.when(native)
     def _():
@@ -148,18 +157,19 @@
         ).wait_recv()
 
     def piece(source, p):
-        return x_all.at[pl.ds(pl.multiple_of(source * ROWS + p * PIECE, PIECE), PIECE), :]
+        start = source // 2 * (2 * ROWS) + p // 2 * ROWS + lax.rem(source, 2) * KS + p % 2 * PIECE
+        return x_all.at[pl.ds(pl.multiple_of(start, PIECE), PIECE), :]
 
     def source_of(dy, dz, dc):
         nz = zq if dz == 0 else 1 - zq
         return lax.rem(y - dy + 4, 4) * 4 + nz * 2 + (core if dc == 0 else 1 - core)
 
     to = tuple(jnp.where(native, a, b) for a, b in zip(near, outer))
-    target = y * 4 + jnp.where(native, zq, z_outer // 4) * 2 + 1 - core
+    target = (y * 2 + jnp.where(native, zq, z_outer // 4)) * (2 * ROWS) + (1 - core) * KS
     for half in (0, 1):
         send(
             swap_out.at[pl.ds(half * PIECE, PIECE), :],
-            x_all.at[pl.ds(pl.multiple_of(target * ROWS + away * KS + half * PIECE, PIECE), PIECE), :],
+            x_all.at[pl.ds(pl.multiple_of(target + away * ROWS + half * PIECE, PIECE), PIECE), :],
             x_send.at[half], x_recv.at[(2 * away + half) * 16], to,
         )
 
@@ -190,15 +200,14 @@
                     c_send.at[index], c_recv.at[index], across(step),
                 )
 
-    def relay_centers(it):
-        for step, slot, half in ((1, 1, 0), (-1, 2, 1)):
-            rows = pl.ds(slot * KS + half * 64, 64)
-            arrived(cen.at[it, rows, :], c_recv.at[it * 6 + (slot - 1) * 2 + half])
-            index = it * 6 + 4 + half
-            send(
-                cen.at[it, rows, :], cen.at[it, pl.ds(3 * KS + half * 64, 64), :],
-                c_send.at[index], c_recv.at[index], across(step),
-            )
+    def relay_center(it, slot, half):
+        rows = pl.ds(slot * KS + half * 64, 64)
+        arrived(cen.at[it, rows, :], c_recv.at[it * 6 + (slot - 1) * 2 + half])
+        index = it * 6 + 4 + half
+        send(
+            cen.at[it, rows, :], cen.at[it, pl.ds(3 * KS + half * 64, 64), :],
+            c_send.at[index], c_recv.at[index], across(1 if slot == 1 else -1),
+        )
 
     def norms(it, q):
         c = cen[it, pl.ds(q * KS, KS), :].astype(F32)
@@ -354,14 +363,38 @@
     mine = cen.at[0, pl.ds(0, KS), :]
     seen = {}
     ready = []
-    phase = 0
+    blocks = 0
     for number, key in enumerate(order):
+        if blocks == 7 and ready:
+            score_chunk(ready.pop(0))
         if key[0] == "relay":
             p = key[1]
             step = 2 if p % 2 == 0 else -2
             arrived(relay_x.at[p], r_recv.at[p])
             origin = y * 4 + lax.rem(z - step + 8, 8) // 4 * 2 + core
             send(relay_x.at[p], piece(origin, p), r_send.at[4 + p], x_recv.at[sem_of((p, 0, 1, 0))], up(0, step, core))
+            continue
+        if key[0] == "mirror":
+
+            @pl.when(foreign)
+            def _():
+                arrived(mine, f_recv.at[0])
+
+            send_centers(0, mine)
+            norms(0, 0)
+            blocks += 1
+            continue
+        if key[0] == "cen":
+            slot, half = key[1:]
+            rows = pl.ds(slot * KS + half * 64, 64)
+            if (slot, half) in ((1, 0), (2, 1)):
+                relay_center(0, slot, half)
+            else:
+                arrived(cen.at[0, rows, :], c_recv.at[(slot - 1) * 2 + half])
+            blocks += 1
+            if blocks == 7:
+                for q in (1, 2, 3):
+                    norms(0, q)
             continue
         p, dy, dz, dc = key
         source = source_of(dy, dz, dc)
@@ -380,37 +413,16 @@
             else:
                 to = up(0, 0, 1 - core) if link == "c" else up(1 if link == "y+" else -1, 0, core)
                 send(piece(source, p), piece(source, p), x_send.at[len(started)], x_recv.at[sem_of(goal)], to)
-        seen[(dy, dz, dc)] = seen.get((dy, dz, dc), 0) + 1
-        if seen[(dy, dz, dc)] == PIECES:
-            ready.append(source)
-        if key == (3, 0, 0, 0):
+        if key == MIRROR_AFTER:
 
             @pl.when(foreign)
             def _():
                 foreign_centers().start()
 
-        if number >= AT[0] and phase == 0:
-
-            @pl.when(foreign)
-            def _():
-                arrived(mine, f_recv.at[0])
-
-            send_centers(0, mine)
-            norms(0, 0)
-            phase = 1
-        if number >= AT[1] and phase == 1:
-            relay_centers(0)
-            phase = 2
-        if number >= AT[2] and phase == 2:
-            for index in (1, 2, 4, 5):
-                slot, half = ((index // 2) + 1, index % 2) if index < 4 else (3, index - 4)
-                arrived(cen.at[0, pl.ds(slot * KS + half * 64, 64), :], c_recv.at[index])
-            for q in (1, 2, 3):
-                norms(0, q)
-            phase = 3
-        if phase == 3:
-            if ready:
-                score_chunk(ready.pop(0))
+        chunk = (dy, dz, p // 2)
+        seen[chunk] = seen.get(chunk, 0) + 1
+        if seen[chunk] == PIECES:
+            ready.append(source // 2 * 2 + p // 2)
     for r in ready:
         score_chunk(r)
     lse = exchange_lse(0)
@@ -420,7 +432,8 @@
     own = cen.at[1, pl.ds(0, KS), :]
     send_centers(1, own)
     score_block(1, 0)
-    relay_centers(1)
+    relay_center(1, 1, 0)
+    relay_center(1, 2, 1)
     for slot in (1, 2):
         half = 2 - slot
         arrived(cen.at[1, pl.ds(slot * KS + half * 64, 64), :], c_recv.at[6 + (slot - 1) * 2 + half])

time: 128 us -> 121 us (0.945); the launches traced: 126 us -> 121 us
  Pallas kernels: 124 us -> 119 us
    pallas_call x1, Pallas kernels: 124 us -> 119 us  [local(): pl.pallas_call(kernel, out_shape=jax.ShapeDtypeStruct((KS, D), jnp.bfloat...]
where the time goes in v4:
time: 121 us
  Pallas kernels  119 us (98%)
  local copies, waits for them, and re-layouts  1.62 us (1%)
    pallas_call x1, Pallas kernels, local(): pl.pallas_call(kernel, out_shape=jax.ShapeDtypeStruct((KS, D), jnp.bfloat...  119 us

profile of v4, /device:TPU:1, one launch (start us, length us, event | category | flops | bytes accessed | tf_op | source)
XLA Modules:
  0.0 120.8 jit_solution(15643485228852230625)
XLA Ops:
  0.0 119.2 %refine.1 = bf16[128,768]{1,0:T(8,128)(2,1)} custom-call(bf16[256,768]{1,0:T(8,128)(2,1)} %vec_ref.1, s32[2]{0:T(128)} %sides_ref.1, bf16[128,768]{1,0:T(8,128)(2,1)} %cen_ref.1), custom_call_target="tpu_custom_call" | custom-call | tf_op jit(solution)/shard_map/refine/pallas_call | solution.py:477
  119.2 1.6 %copy.5 = bf16[128,768]{1,0:T(8,128)(2,1)} copy(bf16[128,768]{1,0:T(8,128)(2,1)} %refine.1) | data formatting | bytes 393216

commit v5 on v4

--- a/solution.py
+++ b/solution.py
@@ -79,10 +79,11 @@
 
 
 def kernel(
-    vec_ref, sides_ref, cen_ref, out_ref,
-    x_all, xt_all, swap_out, keep_out, relay_x, fin, cen, hn, e_all, m_all, l_all, f_one, den_acc, lse_two, lse_all, num, num_low,
+    vec_any, sides_ref, cen_any, out_ref,
+    vec_ref, cen_ref,
+    x_all, xt_all, swap_out, keep_out, relay_x, fin, cen, hn, e_all, m_all, l_all, f_one, den_acc, lse_two, lse_all, lse_sum, num, num_low,
     relay_f32, main_f32, relay_low, main_low, den_out, den_in,
-    x_send, x_recv, go_sem, r_send, r_recv, f_send, f_recv, c_send, c_recv, l_send, l_recv, n_send, n_recv, d_send, d_recv,
+    x_send, x_recv, go_sem, in_sem, r_send, r_recv, f_send, f_recv, c_send, c_recv, l_send, l_recv, n_send, n_recv, d_send, d_recv,
 ):
     wide = lax.axis_index("wide")
     narrow = lax.axis_index("narrow")
@@ -119,6 +120,19 @@
     second = device(0, y, z_second, core)
     mirror = device(0, y, z_second, 1 - core)
 
+    vec_in = pltpu.make_async_copy(vec_any, vec_ref, in_sem.at[0])
+    cen_in = pltpu.make_async_copy(cen_any, cen_ref, in_sem.at[1])
+    vec_in.start()
+    cen_in.start()
+    barrier = pltpu.get_barrier_semaphore()
+
+    around = [up(dy, 0, core) for dy in (1, -1)] + [across(1), across(-1), up(0, 0, 1 - core)]
+    around += [up(0, dz, c) for dz in (1, -1) for c in (core, 1 - core)]
+    for other in around:
+        pl.semaphore_signal(barrier, inc=1, device_id=other, device_id_type=MESH)
+    vec_in.wait()
+    cen_in.wait()
+
     first = vec_ref[0:KS, :]
     other_half = vec_ref[KS : 2 * KS, :]
     first_stays = sides_ref[0] == parity
@@ -131,12 +145,6 @@
         x_all[pl.ds(base, KS), :] = keep_out[...]
         cen[0, 0:KS, :] = cen_ref[...]
 
-    barrier = pltpu.get_barrier_semaphore()
-
-    around = [up(dy, 0, core) for dy in (1, -1)] + [across(1), across(-1), up(0, 0, 1 - core)]
-    around += [up(0, dz, c) for dz in (1, -1) for c in (core, 1 - core)]
-    for other in around:
-        pl.semaphore_signal(barrier, inc=1, device_id=other, device_id_type=MESH)
     pl.semaphore_wait(barrier, len(around))
     for dz in (1, -1):
         pl.semaphore_signal(go_sem, inc=1, device_id=up(0, dz, core), device_id_type=MESH)
@@ -228,10 +236,7 @@
         for q in range(4):
             exponents(q, r, jnp.dot(cen[0, pl.ds(q * KS, KS), :], xt_all[r], preferred_element_type=F32))
 
-    def score_block(it, q, count=1):
-        for k in range(count):
-            norms(it, q + k)
-
+    def score_rows(it, q, count, part):
         def one(g, carry):
             for j in range(UNROLL):
                 r = g * UNROLL + j
@@ -242,49 +247,76 @@
                     exponents(q + k, r, product[k * KS : (k + 1) * KS, :])
             return carry
 
-        lax.fori_loop(0, SRC // UNROLL, one, 0)
+        groups = SRC // UNROLL
+        first, last = (0, groups) if part is None else (part * groups // 2, (part + 1) * groups // 2)
+        lax.fori_loop(first, last, one, 0)
+
+    def score_block(it, q, count=1):
+        for k in range(count):
+            norms(it, q + k)
+        score_rows(it, q, count, None)
 
     def log_add(parts):
         best = functools.reduce(jnp.maximum, parts)
         return best + jnp.log2(sum(jnp.exp2(part - best) for part in parts))
 
-    def lse_copy(it, k):
+    def lines(part):
+        return slice(0, SRC) if part is None else slice(part * 8, part * 8 + 8)
+
+    def lse_copy(it, part, k):
         other = lax.rem(me // 2 + k, SRC // 2)
+        there = lse_all.at[it, me // 2, lines(part), :]
         return pltpu.make_async_remote_copy(
-            src_ref=lse_all.at[it, me // 2], dst_ref=lse_all.at[it, me // 2],
-            send_sem=l_send.at[it, k], recv_sem=l_recv.at[it, me // 2],
+            src_ref=there, dst_ref=there,
+            send_sem=l_send.at[it, (part or 0) * 8 + k], recv_sem=l_recv.at[it, (part or 0) * 9 + me // 2],
             device_id=peer(other * 2 + core), device_id_type=MESH,
         )
 
-    def exchange_lse(it):
-        top = jnp.maximum(jnp.maximum(m_all[0], m_all[1]), jnp.maximum(m_all[2], m_all[3]))
-        total = sum(l_all[q] * jnp.exp2(m_all[q] - top) for q in range(4))
-        lse_two[it, 0] = top + jnp.log2(total)
-        send(lse_two.at[it, 0], lse_two.at[it, 1], l_send.at[it, 0], l_recv.at[it, SRC // 2], up(0, 0, 1 - core))
-        arrived(lse_two.at[it, 1], l_recv.at[it, SRC // 2])
-        lse_all[it, me // 2] = log_add([lse_two[it, 0], lse_two[it, 1]])
+    def lse_start(it, part):
+        at = lines(part)
+        tops = [m_all[q, at, :] for q in range(4)]
+        top = functools.reduce(jnp.maximum, tops)
+        total = sum(l_all[q, at, :] * jnp.exp2(tops[q] - top) for q in range(4))
+        lse_two[it, 0, at, :] = top + jnp.log2(total)
+        send(
+            lse_two.at[it, 0, at, :], lse_two.at[it, 1, at, :],
+            l_send.at[it, (part or 0) * 8], l_recv.at[it, (part or 0) * 9 + 8], up(0, 0, 1 - core),
+        )
+
+    def lse_tell(it, part):
+        at = lines(part)
+        arrived(lse_two.at[it, 1, at, :], l_recv.at[it, (part or 0) * 9 + 8])
+        lse_all[it, me // 2, at, :] = log_add([lse_two[it, 0, at, :], lse_two[it, 1, at, :]])
 
         def tell(k, carry):
-            lse_copy(it, k).start()
+            lse_copy(it, part, k).start()
             return carry
 
         lax.fori_loop(1, SRC // 2, tell, 0)
+
+    def lse_hear(it, part):
+        at = lines(part)
 
         def hear(k, carry):
             other = lax.rem(me // 2 + k, SRC // 2)
-            arrived(lse_all.at[it, other], l_recv.at[it, other])
+            arrived(lse_all.at[it, other, at, :], l_recv.at[it, (part or 0) * 9 + other])
             return carry
 
         lax.fori_loop(1, SRC // 2, hear, 0)
-        return log_add([lse_all[it, k] for k in range(SRC // 2)])
-
-    def weigh(it, q, lse, count=1):
+        lse_sum[it, at, :] = log_add([lse_all[it, k, at, :] for k in range(SRC // 2)])
+
+    def weigh(it, q, count=1, late=None):
         blocks = range(count)
-        for k in blocks:
-            f_one[q + k] = jnp.exp2(m_all[q + k] - lse)
+
+        def factors(part):
+            at = lines(part)
+            for k in blocks:
+                f_one[q + k, at, :] = jnp.exp2(m_all[q + k, at, :] - lse_sum[it, at, :])
+
+        factors(None if late is None else 0)
 
         def group(g, first):
-            lines = []
+            rolls = []
             for k in blocks:
                 parts = []
                 den = jnp.zeros((KS, 128), F32)
@@ -294,10 +326,10 @@
                     wide_weights = weights.astype(F32)
                     den = den + wide_weights[:, :128] + wide_weights[:, 128:]
                     parts.append(weights)
-                lines.append(jnp.concatenate(parts, axis=1))
+                rolls.append(jnp.concatenate(parts, axis=1))
                 den_acc[q + k] = den if first else den_acc[q + k] + den
             rows = x_all[pl.ds(pl.multiple_of(g * 4 * CHUNK, 4 * CHUNK), 4 * CHUNK), :]
-            weights = lines[0] if count == 1 else jnp.concatenate(lines, axis=0)
+            weights = rolls[0] if count == 1 else jnp.concatenate(rolls, axis=0)
             term = jnp.dot(weights, rows, preferred_element_type=F32)
             for k in blocks:
                 part = term[k * KS : (k + 1) * KS, :]
@@ -309,7 +341,13 @@
             group(g, False)
             return carry
 
-        lax.fori_loop(1, 4, one, 0)
+        if late is None:
+            lax.fori_loop(1, 4, one, 0)
+        else:
+            group(1, False)
+            late()
+            factors(1)
+            lax.fori_loop(2, 4, one, 0)
         here = lax.broadcasted_iota(jnp.int32, (KS, 128), 0) == lax.broadcasted_iota(jnp.int32, (KS, 128), 1)
         for k in blocks:
             column = jnp.sum(den_acc[q + k], axis=1, keepdims=True)
@@ -318,9 +356,9 @@
             if LOW[it] and q + k > 0:
                 num_low[it, q + k] = num[it, q + k].astype(BF16)
 
-    def reduce_centers(it, lse, old):
+    def reduce_centers(it, old, late=None):
         table, relay_in, main_in = (num_low, relay_low, main_low) if LOW[it] else (num, relay_f32, main_f32)
-        weigh(it, 3, lse)
+        weigh(it, 3, late=late)
         base = it * 6
         for i, (half, step) in enumerate(((0, 1), (1, -1))):
             send(
@@ -328,7 +366,7 @@
                 n_send.at[base + i], n_recv.at[base + i], across(step),
             )
         send(den_out.at[it, 3], den_in.at[it, 3], d_send.at[it * 4 + 3], d_recv.at[it * 4 + 3], across(2))
-        weigh(it, 1, lse, 2)
+        weigh(it, 1, 2)
         for i, (q, step, half) in enumerate(((2, 1, 1), (1, -1, 0))):
             send(
                 table.at[it, q, pl.ds(half * 64, 64), :], main_in.at[it, i, pl.ds(half * 64, 64), :],
@@ -344,7 +382,7 @@
                 table.at[it, q, rows, :], main_in.at[it, i, rows, :],
                 n_send.at[base + 4 + i], n_recv.at[base + 4 + i], across(step),
             )
-        weigh(it, 0, lse)
+        weigh(it, 0)
         for i, half in enumerate((1, 0)):
             rows = pl.ds(half * 64, 64)
             arrived(main_in.at[it, i, rows, :], n_recv.at[base + 2 + i])
@@ -425,8 +463,10 @@
             ready.append(source // 2 * 2 + p // 2)
     for r in ready:
         score_chunk(r)
-    lse = exchange_lse(0)
-    fresh = reduce_centers(0, lse, mine)
+    lse_start(0, None)
+    lse_tell(0, None)
+    lse_hear(0, None)
+    fresh = reduce_centers(0, mine)
 
     cen[1, 0:KS, :] = fresh
     own = cen.at[1, pl.ds(0, KS), :]
@@ -440,9 +480,15 @@
     score_block(1, 1, 2)
     for half in (0, 1):
         arrived(cen.at[1, pl.ds(3 * KS + half * 64, 64), :], c_recv.at[6 + 4 + half])
-    score_block(1, 3)
-    lse = exchange_lse(1)
-    fin[...] = reduce_centers(1, lse, own)
+    norms(1, 3)
+    score_rows(1, 3, 1, 0)
+    lse_start(1, 0)
+    score_rows(1, 3, 1, 1)
+    lse_tell(1, 0)
+    lse_start(1, 1)
+    lse_tell(1, 1)
+    lse_hear(1, 0)
+    fin[...] = reduce_centers(1, own, lambda: lse_hear(1, 1))
 
     @pl.when(native)
     def _():
@@ -461,10 +507,10 @@
 
     for copy in started:
         copy.wait_send()
-    for it in range(ITERS):
+    for it, part in ((0, None), (1, 0), (1, 1)):
 
         def told(k, carry):
-            lse_copy(it, k).wait_send()
+            lse_copy(it, part, k).wait_send()
             return carry
 
         lax.fori_loop(1, SRC // 2, told, 0)
@@ -477,9 +523,11 @@
     return pl.pallas_call(
         kernel,
         out_shape=jax.ShapeDtypeStruct((KS, D), jnp.bfloat16),
-        in_specs=[whole, pl.BlockSpec(memory_space=pltpu.SMEM), whole],
+        in_specs=[pl.BlockSpec(memory_space=pl.ANY), pl.BlockSpec(memory_space=pltpu.SMEM), pl.BlockSpec(memory_space=pl.ANY)],
         out_specs=whole,
         scratch_shapes=[
+            vmem((2 * KS, D), jnp.bfloat16),
+            vmem((KS, D), jnp.bfloat16),
             vmem((SRC * ROWS, D), jnp.bfloat16),
             vmem((SRC, D, CHUNK), jnp.bfloat16),
             vmem((KS, D), jnp.bfloat16),
@@ -495,6 +543,7 @@
             vmem((4, KS, 128), F32),
             vmem((ITERS, 2, SRC, CHUNK), F32),
             vmem((ITERS, SRC // 2, SRC, CHUNK), F32),
+            vmem((ITERS, SRC, CHUNK), F32),
             vmem((ITERS, 4, KS, D), F32),
             vmem((ITERS, 4, KS, D), BF16),
             vmem((ITERS, 2, 64, D), F32),
@@ -504,11 +553,11 @@
             vmem((ITERS, 4, 8, 128), F32),
             vmem((ITERS, 4, 8, 128), F32),
             dma((160,)), dma((64,)),
-            pltpu.SemaphoreType.REGULAR,
+            pltpu.SemaphoreType.REGULAR, dma((2,)),
             dma((8,)), dma((4,)),
             dma((4,)), dma((2,)),
             dma((6 * ITERS,)), dma((6 * ITERS,)),
-            dma((ITERS, SRC)), dma((ITERS, SRC)),
+            dma((ITERS, SRC)), dma((ITERS, 18)),
             dma((6 * ITERS,)), dma((6 * ITERS,)),
             dma((4 * ITERS,)), dma((4 * ITERS,)),
         ],

time: 121 us -> 120 us (level)
  no operation moved by 1% of the time
where the time goes in v5:
time: 120 us
  Pallas kernels  118 us (98%)
  local copies, waits for them, and re-layouts  1.62 us (1%)
    pallas_call x1, Pallas kernels, local(): pl.pallas_call(kernel, out_shape=jax.ShapeDtypeStruct((KS, D), jnp.bfloat...  118 us

profile of v5, /device:TPU:1, one launch (start us, length us, event | category | flops | bytes accessed | tf_op | source)
XLA Modules:
  0.0 119.7 jit_solution(13555794083403220307)
XLA Ops:
  0.0 118.1 %refine.1 = bf16[128,768]{1,0:T(8,128)(2,1)} custom-call(bf16[256,768]{1,0:T(8,128)(2,1)} %vec_any.1, s32[2]{0:T(128)} %sides_ref.1, bf16[128,768]{1,0:T(8,128)(2,1)} %cen_any.1), custom_call_target="tpu_custom_call" | custom-call | tf_op jit(solution)/shard_map/refine/pallas_call | solution.py:523
  118.1 1.6 %copy.5 = bf16[128,768]{1,0:T(8,128)(2,1)} copy(bf16[128,768]{1,0:T(8,128)(2,1)} %refine.1) | data formatting | bytes 393216

commit v6 on v5

--- a/solution.py
+++ b/solution.py
@@ -35,13 +35,13 @@
     out = []
     if dc == 1:
         return out
-    if dy == 0 and dz == 0:
-        out.append(("z+" if p % 2 == 0 else "z-", ("relay", p)))
     relay = 1 if (p + dz) % 2 == 0 else -1
     if dy == 0:
         out += [("y+", (p, 1, dz, 0)), ("y-", (p, 3, dz, 0))]
     elif (dy == 1 and relay == 1) or (dy == 3 and relay == -1):
         out.append(("y+" if relay == 1 else "y-", (p, 2, dz, 0)))
+    if dy == 0 and dz == 0:
+        out.append(("z+" if p % 2 == 0 else "z-", ("relay", p)))
     out.append(("c", (p, dy, dz, 1)))
     return out
 
@@ -148,7 +148,6 @@
     pl.semaphore_wait(barrier, len(around))
     for dz in (1, -1):
         pl.semaphore_signal(go_sem, inc=1, device_id=up(0, dz, core), device_id_type=MESH)
-    pl.semaphore_wait(go_sem, 2)
 
     started = []
 
@@ -195,6 +194,7 @@
 
     @pl.when(foreign)
     def _():
+        pl.semaphore_wait(go_sem, 2)
         foreign_rows(0).start()
         foreign_rows(1).start()
 
@@ -446,6 +446,12 @@
             arrived(piece(source, p), x_recv.at[sem_of(key)])
         for link, goal in sends(key):
             if goal[0] == "relay":
+                if key == (0, 0, 0, 0):
+
+                    @pl.when(native)
+                    def _():
+                        pl.semaphore_wait(go_sem, 2)
+
                 step = 2 if p % 2 == 0 else -2
                 send(piece(source, p), relay_x.at[p], r_send.at[p], r_recv.at[p], up(0, step, core))
             else:

time: 120 us -> 123 us (1.025)
  Pallas kernels: 118 us -> 121 us
    pallas_call x1, Pallas kernels: 118 us -> 121 us  [local(): pl.pallas_call(kernel, out_shape=jax.ShapeDtypeStruct((KS, D), jnp.bfloat...]
where the time goes in v6:
time: 123 us
  Pallas kernels  121 us (98%)
  local copies, waits for them, and re-layouts  1.62 us (1%)
    pallas_call x1, Pallas kernels, local(): pl.pallas_call(kernel, out_shape=jax.ShapeDtypeStruct((KS, D), jnp.bfloat...  121 us

profile of v6, /device:TPU:1, one launch (start us, length us, event | category | flops | bytes accessed | tf_op | source)
XLA Modules:
  0.0 123.0 jit_solution(6339591349637557818)
XLA Ops:
  0.0 121.4 %refine.1 = bf16[128,768]{1,0:T(8,128)(2,1)} custom-call(bf16[256,768]{1,0:T(8,128)(2,1)} %vec_any.1, s32[2]{0:T(128)} %sides_ref.1, bf16[128,768]{1,0:T(8,128)(2,1)} %cen_any.1), custom_call_target="tpu_custom_call" | custom-call | tf_op jit(solution)/shard_map/refine/pallas_call | solution.py:529
  121.4 1.6 %copy.5 = bf16[128,768]{1,0:T(8,128)(2,1)} copy(bf16[128,768]{1,0:T(8,128)(2,1)} %refine.1) | data formatting | bytes 393216

commit v7 on v5

--- a/solution.py
+++ b/solution.py
@@ -148,7 +148,6 @@
     pl.semaphore_wait(barrier, len(around))
     for dz in (1, -1):
         pl.semaphore_signal(go_sem, inc=1, device_id=up(0, dz, core), device_id_type=MESH)
-    pl.semaphore_wait(go_sem, 2)
 
     started = []
 
@@ -192,6 +191,8 @@
             src_ref=cen_ref, dst_ref=cen.at[0, pl.ds(0, KS), :], send_sem=f_send.at[2], recv_sem=f_recv.at[0],
             device_id=mirror, device_id_type=MESH,
         )
+
+    pl.semaphore_wait(go_sem, 2)
 
     @pl.when(foreign)
     def _():

time: 120 us -> 123 us (1.025)
  Pallas kernels: 118 us -> 121 us
    pallas_call x1, Pallas kernels: 118 us -> 121 us  [local(): pl.pallas_call(kernel, out_shape=jax.ShapeDtypeStruct((KS, D), jnp.bfloat...]
where the time goes in v7:
time: 123 us
  Pallas kernels  121 us (98%)
  local copies, waits for them, and re-layouts  1.62 us (1%)
    pallas_call x1, Pallas kernels, local(): pl.pallas_call(kernel, out_shape=jax.ShapeDtypeStruct((KS, D), jnp.bfloat...  121 us

profile of v7, /device:TPU:1, one launch (start us, length us, event | category | flops | bytes accessed | tf_op | source)
XLA Modules:
  0.0 123.0 jit_solution(2770283081132294305)
XLA Ops:
  0.0 121.4 %refine.1 = bf16[128,768]{1,0:T(8,128)(2,1)} custom-call(bf16[256,768]{1,0:T(8,128)(2,1)} %vec_any.1, s32[2]{0:T(128)} %sides_ref.1, bf16[128,768]{1,0:T(8,128)(2,1)} %cen_any.1), custom_call_target="tpu_custom_call" | custom-call | tf_op jit(solution)/shard_map/refine/pallas_call | solution.py:524
  121.4 1.6 %copy.5 = bf16[128,768]{1,0:T(8,128)(2,1)} copy(bf16[128,768]{1,0:T(8,128)(2,1)} %refine.1) | data formatting | bytes 393216
